TPU v7x, 256 devices: a whole 4x4x8 slice. The times are simulated.
256 devices in a mesh: tx: 32 (over z, y), ty: 8 (over x, core).
Axes of the slice: x: 4, y: 4, z: 8, core: 2. Of those that a mesh axis runs over, the one named last changes fastest.
Arguments:
- probes: bfloat16 [4096, 1024, 128], P('tx', 'ty')
- filter_taps: float32 [2, 2, 33], replicated, may hold values from 0.05 to 1
- cluster_ranks: int32 [5, 32, 8], replicated, may hold values from 64 to 128
Outputs:
- leaf_basis: bfloat16 [4096, 1024, 128], P('tx', 'ty')
- transfers: float32 [32, 8, 4, 128, 128], P('tx', 'ty')
Inputs may be any that keep to these rules, and one draw needn't show every extreme that they name: `cluster_ranks`: only the entry of a cluster's first leaf (lowest row and column indices) is its rank at that level.
All inputs are finite; a program needn't handle non-finite values.
Results may differ from a plain program's by a relative error of at most 0.014.
The roundings to bfloat16 on the way count: a program that leaves them out, or rounds other values in their place, can miss the bound.
Values may be sent and summed in bfloat16 or wider, within the bound.
A program may use at most 128 MiB of HBM per device.

v0:
```python
import jax
import jax.numpy as jnp
from jax import lax
from jax.sharding import PartitionSpec as P


def extended(block, sides, width):
    for axis, dim in sides:
        count = lax.axis_size(axis)
        forward = [(i, i + 1) for i in range(count - 1)]
        backward = [(target, source) for source, target in forward]
        low = lax.ppermute(
            lax.slice_in_dim(block, block.shape[dim] - width, None, axis=dim), axis, forward
        )
        high = lax.ppermute(lax.slice_in_dim(block, 0, width, axis=dim), axis, backward)
        block = jnp.concatenate([low, block, high], axis=dim)
    return block


def from_partner(shard, axis, stride):
    return lax.ppermute(shard, axis, [(i, i ^ 1 << stride) for i in range(lax.axis_size(axis))])


def solve_triangular(matrix, right):
    return jax.scipy.linalg.solve_triangular(matrix, right, lower=True)


def composite(filter_taps):
    count = filter_taps.shape[-1]
    wide = 5 * (count - 1) + 1
    first = jnp.arange(count)[:, None, None]
    second = jnp.arange(count)[None, :, None]
    spot = jnp.arange(wide)[None, None, :]
    table = (first + 4 * second == spot).astype(jnp.float32)
    outer = filter_taps[:, 0, :, None] * filter_taps[:, 1, None, :]
    return jnp.einsum("dab,abm->dm", outer, table, precision=lax.Precision.HIGHEST).astype(
        jnp.bfloat16
    )


def toeplitz(line_taps, length):
    wide = line_taps.shape[0]
    columns = length + wide - 1
    pattern = jnp.concatenate([line_taps, jnp.zeros((length,), line_taps.dtype)])
    return jnp.tile(pattern, length)[: length * columns].reshape(length, columns)


def factor(gram, keep_mask):
    outer = keep_mask[..., :, None] * keep_mask[..., None, :]
    masked = gram * outer
    trace_sum = jnp.sum(jnp.diagonal(masked, axis1=-2, axis2=-1), axis=-1)
    delta = 0.01 * trace_sum / jnp.sum(keep_mask, axis=-1)
    ident = jnp.eye(gram.shape[-1], dtype=jnp.float32)
    shifted = (
        masked
        + ident * (1.0 - keep_mask)[..., None, :]
        + delta[..., None, None] * ident * keep_mask[..., None, :]
    )
    return (masked, jnp.linalg.cholesky(shifted))


def products(zeta):
    return jnp.einsum("...kp,...kq->...pq", zeta, zeta, precision=lax.Precision.HIGHEST)


def transfer(lower, keep_mask, child_z):
    right = keep_mask[..., :, None] * jnp.swapaxes(child_z, -1, -2)
    return jnp.swapaxes(solve_triangular(lower, right), -1, -2)


def rank_mask(rank_value, width):
    return (jnp.arange(width) < rank_value[..., None]).astype(jnp.float32)


def climb_level(child_z, own_gram, partner_gram, keep_mask):
    merged = (own_gram + partner_gram) * 0.5
    masked, lower = factor(merged, keep_mask)
    moved = transfer(lower, keep_mask, child_z)
    zeta = solve_triangular(lower, masked)
    return (moved, zeta, products(zeta))


def local(probes, filter_taps, cluster_ranks):
    combined = composite(filter_taps)
    reach = (combined.shape[1] - 1) // 2
    rows, cols, width = probes.shape
    tall = extended(probes, (("tx", 0),), reach)
    middle = jnp.dot(
        toeplitz(combined[0], rows),
        tall.reshape(tall.shape[0], cols * width),
        preferred_element_type=jnp.float32,
    )
    middle = middle.reshape(rows, cols, width).astype(jnp.bfloat16)
    broad = extended(middle, (("ty", 1),), reach)
    sketch = jnp.einsum(
        "yc,xcp->xyp", toeplitz(combined[1], cols), broad, preferred_element_type=jnp.float32
    ).astype(jnp.bfloat16)
    flat = sketch.reshape(rows * cols, width)
    gram = jnp.einsum("np,nq->pq", flat, flat, preferred_element_type=jnp.float32) / (rows * cols)
    row_at = lax.axis_index("tx")
    col_at = lax.axis_index("ty")
    keep_mask = rank_mask(cluster_ranks[0, row_at, col_at], width)
    masked, lower = factor(gram, keep_mask)
    diag_mask = jnp.eye(width, dtype=jnp.float32) * keep_mask[None, :]
    weights = jnp.swapaxes(solve_triangular(lower, diag_mask), -1, -2).astype(jnp.bfloat16)
    leaf_basis = (
        jnp.dot(flat, weights, preferred_element_type=jnp.float32)
        .astype(jnp.bfloat16)
        .reshape(rows, cols, width)
    )
    zeta = solve_triangular(lower, masked)
    grams = products(zeta)
    row_two = row_at - row_at % 2
    row_four = row_at - row_at % 4
    col_two = col_at - col_at % 2
    col_four = col_at - col_at % 4
    partner = from_partner(grams, "tx", 0)
    first_e, zeta, grams = climb_level(
        zeta, grams, partner, rank_mask(cluster_ranks[1, row_two, col_at], width)
    )
    partner = from_partner(grams, "ty", 0)
    second_e, zeta, grams = climb_level(
        zeta, grams, partner, rank_mask(cluster_ranks[2, row_two, col_two], width)
    )
    partner = from_partner(grams, "tx", 1)
    third_e, zeta, grams = climb_level(
        zeta, grams, partner, rank_mask(cluster_ranks[3, row_four, col_two], width)
    )
    partner = from_partner(grams, "ty", 1)
    fourth_e, zeta, grams = climb_level(
        zeta, grams, partner, rank_mask(cluster_ranks[4, row_four, col_four], width)
    )
    transfers = jnp.stack([first_e, second_e, third_e, fourth_e], axis=0)[None, None]
    return (leaf_basis, transfers)


def solution(mesh):
    in_specs = (P("tx", "ty", None), P(), P())
    out_specs = (P("tx", "ty", None), P("tx", "ty", None, None, None))
    return jax.shard_map(local, mesh=mesh, in_specs=in_specs, out_specs=out_specs, check_vma=False)
```

profile of v0, /device:TPU:96, one launch (start us, length us, event | category | flops | bytes accessed | tf_op | source)
XLA Modules:
  0.0 307.9 jit_solution(15450062606246432339)
XLA Ops:
  0.6 7.0 %fusion.76 = (bf16[80,128,128]{2,1,0:T(8,128)(2,1)}, bf16[80,128,128]{2,1,0:T(8,128)(2,1)}) fusion(bf16[128,128,128]{2,1,0:T(8,128)(2,1)} %param.6), kind=kLoop, calls=%fused_computation.134 | loop fusion | bytes 10485760 | tf_op jit(solution)/shard_map/slice | solution.py:13
  7.7 4.5 %collective-permute-start.1 = (bf16[80,128,128]{2,1,0:T(8,128)(2,1)}, bf16[80,128,128]{2,1,0:T(8,128)(2,1)S(1)}, u32[]{:S(2)}, u32[]{:S(2)}) collective-permute-start(bf16[80,128,128]{2,1,0:T(8,128)(2,1)} %get-tuple-element.13), channel_id=1, source_target_pairs={{8,0},{16,8},{24,16},{32,24},{40,32},{48,40},{56,48},{64,56},{72,6... | collective-permute-start | bytes 7864328 | tf_op jit(solution)/shard_map/ppermute | solution.py:15
  12.1 1.9 collective-permute-start
  15.4 53.2 %collective-permute-done.1 = bf16[80,128,128]{2,1,0:T(8,128)(2,1)S(1)} collective-permute-done((bf16[80,128,128]{2,1,0:T(8,128)(2,1)}, bf16[80,128,128]{2,1,0:T(8,128)(2,1)S(1)}, u32[]{:S(2)}, u32[]{:S(2)}) %collective-permute-start.1) | collective-permute-done | bytes 2621472 | tf_op jit(solution)/shard_map/ppermute | solution.py:15
  68.5 6.2 %collective-permute-done = bf16[80,128,128]{2,1,0:T(8,128)(2,1)} collective-permute-done((bf16[80,128,128]{2,1,0:T(8,128)(2,1)}, bf16[80,128,128]{2,1,0:T(8,128)(2,1)}, u32[]{:S(2)}, u32[]{:S(2)}) %collective-permute-start) | collective-permute-done | bytes 2621472 | tf_op jit(solution)/shard_map/ppermute | solution.py:12
  74.8 4.3 %pad_maximum_fusion = bf16[288,128,128]{2,1,0:T(8,128)(2,1)S(1)} fusion(bf16[80,128,128]{2,1,0:T(8,128)(2,1)S(1)} %collective-permute-done.1, bf16[128,128,128]{2,1,0:T(8,128)(2,1)} %param.6, bf16[80,128,128]{2,1,0:T(8,128)(2,1)} %collective-permute-done), kind=kLoop, calls=%fused_computation.10 | loop fusion | flops 9437184 | bytes 18874368 | tf_op jit(solution)/shard_map/concatenate | solution.py:16
  79.0 21.2 %fusion.10 = bf16[128,128,128]{2,0,1:T(8,128)(2,1)S(1)} fusion(bf16[128,288]{1,0:T(8,128)(2,1)S(1)} %reshape.135, bf16[36,8,128,128]{3,2,1,0:T(8,128)(2,1)S(1)} %bitcast.157), kind=kOutput, calls=%fused_computation.17 | convolution fusion | flops 1210056704 | bytes 13705216 | tf_op jit(solution)/shard_map/dot_general | solution.py:88
  100.2 3.7 %fusion.75 = (bf16[128,80,128]{2,0,1:T(8,128)(2,1)}, bf16[128,80,128]{2,0,1:T(8,128)(2,1)}) fusion(bf16[128,128,128]{2,0,1:T(8,128)(2,1)S(1)} %fusion.10), kind=kLoop, calls=%fused_computation.133 | loop fusion | bytes 10485760 | tf_op jit(solution)/shard_map/slice | solution.py:13
  105.2 4.7 %collective-permute-start.2 = (bf16[128,80,128]{2,0,1:T(8,128)(2,1)}, bf16[128,80,128]{2,0,1:T(8,128)(2,1)}, u32[]{:S(2)}, u32[]{:S(2)}) collective-permute-start(bf16[128,80,128]{2,0,1:T(8,128)(2,1)} %get-tuple-element.10), channel_id=1, source_target_pairs={{0,1},{1,2},{2,3},{3,4},{4,5},{5,6},{6,7},{8,9},{9,10},{10,11},{11... | collective-permute-start | bytes 7864328 | tf_op jit(solution)/shard_map/ppermute | solution.py:12
  122.2 4.1 %pad_maximum_fusion.1 = bf16[128,288,128]{2,0,1:T(8,128)(2,1)S(1)} fusion(bf16[128,80,128]{2,0,1:T(8,128)(2,1)S(1)} %collective-permute-done.3, bf16[128,128,128]{2,0,1:T(8,128)(2,1)} %copy-done, bf16[128,80,128]{2,0,1:T(8,128)(2,1)} %collective-permute-done.2), kind=kLoop, calls=%fused_computation.11 | loop fusion | flops 9437184 | bytes 18874368 | tf_op jit(solution)/shard_map/concatenate | solution.py:16
  126.3 6.5 %fusion.7 = bf16[128,128,128]{1,2,0:T(8,128)(2,1)S(1)} fusion(bf16[128,288,128]{2,0,1:T(8,128)(2,1)S(1)} %pad_maximum_fusion.1, bf16[128,288]{1,0:T(8,128)(2,1)S(1)} %reshape.137), kind=kOutput, calls=%fused_computation.16 | convolution fusion | flops 1210056704 | bytes 13705216 | tf_op jit(solution)/shard_map/yc,xcp->xyp/dot_general | solution.py:95
  132.9 1.9 copy-done.1
  136.2 1.7 gather_fusion
  140.1 11.7 %cholesky.89 = f32[128,128]{1,0:T(8,128)S(1)} custom-call(f32[128,128]{1,0:T(8,128)S(1)} %fusion.54), custom_call_target="Cholesky" | custom-call | tf_op jit(solution)/shard_map/jit(cholesky)/cholesky | solution.py:59
  153.1 9.8 %custom-call.23 = f32[1,128,128]{1,2,0:T(8,128)S(1)} custom-call(f32[1,128,128]{2,1,0:T(8,128)S(1)} %fusion.28), custom_call_target="InvertDiagBlocksLowerTriangular" | custom-call | tf_op jit(solution)/shard_map/jit(_solve_triangular)/triangular_solve | solution.py:25
  164.0 5.5 %convolution_convert_fusion = bf16[16384,128]{1,0:T(8,128)(2,1)} fusion(bf16[16384,128]{1,0:T(8,128)(2,1)} %bitcast.159, bf16[128,128]{1,0:T(8,128)(2,1)S(1)} %convolution_convert_fusion.1), kind=kOutput, calls=%fused_computation.5 | convolution fusion | flops 538968064 | bytes 8421376 | tf_op jit(solution)/shard_map/dot_general | solution.py:107
  173.3 11.7 %cholesky.100 = f32[128,128]{1,0:T(8,128)S(1)} custom-call(f32[128,128]{1,0:T(8,128)S(1)} %fusion.50), custom_call_target="Cholesky" | custom-call | tf_op jit(solution)/shard_map/jit(cholesky)/cholesky | solution.py:59
  186.4 9.8 %custom-call.25 = f32[1,128,128]{1,2,0:T(8,128)S(1)} custom-call(f32[1,128,128]{2,1,0:T(8,128)S(1)} %fusion.29), custom_call_target="InvertDiagBlocksLowerTriangular" | custom-call | tf_op jit(solution)/shard_map/jit(_solve_triangular)/triangular_solve | solution.py:25
  196.9 16.1 %collective-permute-start.5 = (f32[128,128]{0,1:T(8,128)S(1)}, f32[128,128]{0,1:T(8,128)S(1)}, u32[]{:S(2)}, u32[]{:S(2)}) collective-permute-start(f32[128,128]{0,1:T(8,128)S(1)} %fusion.79), channel_id=1, source_target_pairs={{0,1},{1,0},{2,3},{3,2},{4,5},{5,4},{6,7},{7,6},{8,9},{9,8},{10,11... | collective-permute-start | bytes 196616 | tf_op jit(solution)/shard_map/ppermute | solution.py:21
  214.0 1.5 gather_fusion.2
  217.6 11.7 %cholesky.111 = f32[128,128]{1,0:T(8,128)S(1)} custom-call(f32[128,128]{1,0:T(8,128)S(1)} %fusion.45), custom_call_target="Cholesky" | custom-call | tf_op jit(solution)/shard_map/jit(cholesky)/cholesky | solution.py:59
  230.7 9.8 %custom-call.27 = f32[1,128,128]{1,2,0:T(8,128)S(1)} custom-call(f32[1,128,128]{2,1,0:T(8,128)S(1)} %fusion.30), custom_call_target="InvertDiagBlocksLowerTriangular" | custom-call | tf_op jit(solution)/shard_map/jit(_solve_triangular)/triangular_solve | solution.py:25
  241.2 2.4 collective-permute-start.6
  244.0 3.2 %collective-permute-done.6 = f32[128,128]{0,1:T(8,128)S(1)} collective-permute-done((f32[128,128]{0,1:T(8,128)S(1)}, f32[128,128]{0,1:T(8,128)S(1)}, u32[]{:S(2)}, u32[]{:S(2)}) %collective-permute-start.6) | collective-permute-done | bytes 65568 | tf_op jit(solution)/shard_map/ppermute | solution.py:21
  247.2 1.5 gather_fusion.3
  251.0 11.7 %cholesky.122 = f32[128,128]{1,0:T(8,128)S(1)} custom-call(f32[128,128]{1,0:T(8,128)S(1)} %fusion.40), custom_call_target="Cholesky" | custom-call | tf_op jit(solution)/shard_map/jit(cholesky)/cholesky | solution.py:59
  264.1 9.8 %custom-call.29 = f32[1,128,128]{1,2,0:T(8,128)S(1)} custom-call(f32[1,128,128]{2,1,0:T(8,128)S(1)} %fusion.31), custom_call_target="InvertDiagBlocksLowerTriangular" | custom-call | tf_op jit(solution)/shard_map/jit(_solve_triangular)/triangular_solve | solution.py:25
  274.6 2.7 collective-permute-start.7
  277.6 1.9 collective-permute-done.7
  279.7 1.6 gather_fusion.4
  283.5 11.7 %cholesky.133 = f32[128,128]{1,0:T(8,128)S(1)} custom-call(f32[128,128]{1,0:T(8,128)S(1)} %fusion.35), custom_call_target="Cholesky" | custom-call | tf_op jit(solution)/shard_map/jit(cholesky)/cholesky | solution.py:59
  296.6 9.8 %custom-call.31 = f32[1,128,128]{1,2,0:T(8,128)S(1)} custom-call(f32[1,128,128]{2,1,0:T(8,128)S(1)} %fusion.32), custom_call_target="InvertDiagBlocksLowerTriangular" | custom-call | tf_op jit(solution)/shard_map/jit(_solve_triangular)/triangular_solve | solution.py:25
  (100 shorter events, 34.7 us)
Async XLA Ops:
  0.6 13.4 %copy-start.2 = (f32[2,2,33]{2,1,0:T(2,128)S(1)}, f32[2,2,33]{2,1,0:T(2,128)}, u32[]{:S(2)}) copy-start(f32[2,2,33]{2,1,0:T(2,128)} %param.7) | copy-start | bytes 1588
  7.7 60.9 %collective-permute-start.1 = (bf16[80,128,128]{2,1,0:T(8,128)(2,1)}, bf16[80,128,128]{2,1,0:T(8,128)(2,1)S(1)}, u32[]{:S(2)}, u32[]{:S(2)}) collective-permute-start(bf16[80,128,128]{2,1,0:T(8,128)(2,1)} %get-tuple-element.13), channel_id=1, source_target_pairs={{8,0},{16,8},{24,16},{32,24},{40,32},{48,40},{56,48},{64,56},{72,6... | collective-permute-start | bytes 7864328 | tf_op jit(solution)/shard_map/ppermute | solution.py:15
  12.1 62.6 %collective-permute-start = (bf16[80,128,128]{2,1,0:T(8,128)(2,1)}, bf16[80,128,128]{2,1,0:T(8,128)(2,1)}, u32[]{:S(2)}, u32[]{:S(2)}) collective-permute-start(bf16[80,128,128]{2,1,0:T(8,128)(2,1)} %get-tuple-element.12), channel_id=1, source_target_pairs={{0,8},{8,16},{16,24},{24,32},{32,40},{40,48},{48,56},{56,64},{64,7... | collective-permute-start | bytes 7864328 | tf_op jit(solution)/shard_map/ppermute | solution.py:12
  100.2 3.7 %copy-start = (bf16[128,128,128]{2,0,1:T(8,128)(2,1)}, bf16[128,128,128]{2,0,1:T(8,128)(2,1)S(1)}, u32[]{:S(2)}) copy-start(bf16[128,128,128]{2,0,1:T(8,128)(2,1)S(1)} %fusion.10) | copy-start | bytes 12582916
  103.9 18.3 %collective-permute-start.3 = (bf16[128,80,128]{2,0,1:T(8,128)(2,1)}, bf16[128,80,128]{2,0,1:T(8,128)(2,1)S(1)}, u32[]{:S(2)}, u32[]{:S(2)}) collective-permute-start(bf16[128,80,128]{2,0,1:T(8,128)(2,1)} %get-tuple-element.11), channel_id=1, source_target_pairs={{1,0},{2,1},{3,2},{4,3},{5,4},{6,5},{7,6},{9,8},{10,9},{11,10},{12... | collective-permute-start | bytes 7864328 | tf_op jit(solution)/shard_map/ppermute | solution.py:15
  105.2 17.0 %collective-permute-start.2 = (bf16[128,80,128]{2,0,1:T(8,128)(2,1)}, bf16[128,80,128]{2,0,1:T(8,128)(2,1)}, u32[]{:S(2)}, u32[]{:S(2)}) collective-permute-start(bf16[128,80,128]{2,0,1:T(8,128)(2,1)} %get-tuple-element.10), channel_id=1, source_target_pairs={{0,1},{1,2},{2,3},{3,4},{4,5},{5,6},{6,7},{8,9},{9,10},{10,11},{11... | collective-permute-start | bytes 7864328 | tf_op jit(solution)/shard_map/ppermute | solution.py:12
  132.8 1.9 copy-start.1
  163.9 5.7 %collective-permute-start.4 = (f32[128,128]{0,1:T(8,128)S(1)}, f32[128,128]{0,1:T(8,128)S(1)}, u32[]{:S(2)}, u32[]{:S(2)}) collective-permute-start(f32[128,128]{0,1:T(8,128)S(1)} %fusion.78), channel_id=1, source_target_pairs={{0,8},{8,0},{16,24},{24,16},{32,40},{40,32},{48,56},{56,48},{64,72... | collective-permute-start | bytes 196616 | tf_op jit(solution)/shard_map/ppermute | solution.py:21
  196.9 17.0 %collective-permute-start.5 = (f32[128,128]{0,1:T(8,128)S(1)}, f32[128,128]{0,1:T(8,128)S(1)}, u32[]{:S(2)}, u32[]{:S(2)}) collective-permute-start(f32[128,128]{0,1:T(8,128)S(1)} %fusion.79), channel_id=1, source_target_pairs={{0,1},{1,0},{2,3},{3,2},{4,5},{5,4},{6,7},{7,6},{8,9},{9,8},{10,11... | collective-permute-start | bytes 196616 | tf_op jit(solution)/shard_map/ppermute | solution.py:21
  241.2 5.9 %collective-permute-start.6 = (f32[128,128]{0,1:T(8,128)S(1)}, f32[128,128]{0,1:T(8,128)S(1)}, u32[]{:S(2)}, u32[]{:S(2)}) collective-permute-start(f32[128,128]{0,1:T(8,128)S(1)} %fusion.80), channel_id=1, source_target_pairs={{0,16},{8,24},{16,0},{24,8},{32,48},{40,56},{48,32},{56,40},{64,80... | collective-permute-start | bytes 196616 | tf_op jit(solution)/shard_map/ppermute | solution.py:21
  274.6 5.0 %collective-permute-start.7 = (f32[128,128]{0,1:T(8,128)S(1)}, f32[128,128]{0,1:T(8,128)S(1)}, u32[]{:S(2)}, u32[]{:S(2)}) collective-permute-start(f32[128,128]{0,1:T(8,128)S(1)} %fusion.81), channel_id=1, source_target_pairs={{0,2},{1,3},{2,0},{3,1},{4,6},{5,7},{6,4},{7,5},{8,10},{9,11},{10,... | collective-permute-start | bytes 196616 | tf_op jit(solution)/shard_map/ppermute | solution.py:21
where the time goes:
time: 313 us; the launch traced here: 308 us
  other arithmetic  137 us (44%)
  waiting for transfers between devices  65.1 us (21%)
  matrix products  39 us (12%)
  starting transfers between devices  33.8 us (11%)
  local copies, waits for them, and re-layouts  24.5 us (8%)
  between operations  8.26 us (3%)
    another operation x15, other arithmetic, factor(): return (masked, jnp.linalg.cholesky(shifted))  61.9 us
    ppermute x2, waiting for transfers between devices, extended(): lax.ppermute(lax.slice_in_dim(block, 0, width, axis=dim), axis, backward)  53.2 us
    another operation x10, other arithmetic, solve_triangular(): return jax.scipy.linalg.solve_triangular(matrix, right, lower=True)  52.3 us
    ppermute x4, starting transfers between devices, from_partner(): lax.ppermute(shard, axis, [(i, i ^ 1 << stride) for i in range(lax.axis_s...  21.4 us
    dot_general x1, matrix products, local(): jnp.dot(toeplitz(combined[0], rows), tall.reshape(tall.shape[0], cols * w...  21.2 us
    slice x2, local copies, waits for them, and re-layouts, extended(): lax.slice_in_dim(block, block.shape[dim] - width, None, axis=dim)  10.7 us
    concatenate x2, other arithmetic, extended(): block = jnp.concatenate([low, block, high], axis=dim)  8.37 us
    gather x5, local copies, waits for them, and re-layouts, factor(): trace_sum = jnp.sum(jnp.diagonal(masked, axis1=-2, axis2=-1), axis=-1)  7.74 us
  transfers between devices with their start and end apart: 8, of which 5 were waited for; matrix products, arithmetic and copies ran while one was open for 6% of the time, Pallas kernels for 0%

commit v1 on v0

v1 whole, which is shorter than its diff:
```python
import jax
import jax.numpy as jnp
from jax import lax
from jax.experimental import pallas as pl
from jax.experimental.pallas import tpu as pltpu
from jax.sharding import PartitionSpec as P

HIGHEST = lax.Precision.HIGHEST
F = jnp.float32


def extended(block, sides, width):
    for axis, dim in sides:
        count = lax.axis_size(axis)
        forward = [(i, i + 1) for i in range(count - 1)]
        backward = [(target, source) for source, target in forward]
        low = lax.ppermute(
            lax.slice_in_dim(block, block.shape[dim] - width, None, axis=dim), axis, forward
        )
        high = lax.ppermute(lax.slice_in_dim(block, 0, width, axis=dim), axis, backward)
        block = jnp.concatenate([low, block, high], axis=dim)
    return block


def from_partner(shard, axis, stride):
    return lax.ppermute(shard, axis, [(i, i ^ 1 << stride) for i in range(lax.axis_size(axis))])


def composite(filter_taps):
    count = filter_taps.shape[-1]
    wide = 5 * (count - 1) + 1
    first = jnp.arange(count)[:, None, None]
    second = jnp.arange(count)[None, :, None]
    spot = jnp.arange(wide)[None, None, :]
    table = (first + 4 * second == spot).astype(jnp.float32)
    outer = filter_taps[:, 0, :, None] * filter_taps[:, 1, None, :]
    return jnp.einsum("dab,abm->dm", outer, table, precision=lax.Precision.HIGHEST).astype(
        jnp.bfloat16
    )


def toeplitz(line_taps, length):
    wide = line_taps.shape[0]
    columns = length + wide - 1
    pattern = jnp.concatenate([line_taps, jnp.zeros((length,), line_taps.dtype)])
    return jnp.tile(pattern, length)[: length * columns].reshape(length, columns)


def lane_of(x, i): return jnp.broadcast_to(x[:, i:i+1], (8,128))
def row_of(x, i): return jnp.broadcast_to(x[i:i+1,:], (8,128))

def eliminate(X):
    sub=lax.broadcasted_iota(jnp.int32,(8,128),0); lane=lax.broadcasted_iota(jnp.int32,(8,128),1)
    X=list(X); out=[]
    for b in range(16):
        j=8*b
        head=X[b]
        B=[lane_of(head,j+c) for c in range(8)]
        C={t:[lane_of(X[t],j+c) for c in range(8)] for t in range(b+1,16)}
        inblk=(lane>=j)&(lane<j+8)
        head=jnp.where(inblk,jnp.where(lane-j==sub,1.0,0.0),head)
        V=jnp.zeros((8,128),F)
        for c in range(8):
            d=row_of(B[c],c)
            inv=1.0/d
            prow=row_of(head,c)
            V=jnp.where(sub==c,prow*lax.rsqrt(d),V)
            prow=prow*inv
            col=B[c]
            head=jnp.where(sub==c,prow,head-col*prow)
            for e in range(c+1,8):
                brow=row_of(B[e],c)*inv
                B[e]=jnp.where(sub==c,brow,B[e]-col*brow)
        out.append(jnp.where(lane<=j+sub,V,0.0))
        rows=[row_of(head,c) for c in range(8)]
        for t in range(b+1,16):
            acc=jnp.where(inblk,0.0,X[t])
            p=[C[t][c]*rows[c] for c in range(8)]
            s=((p[0]+p[1])+(p[2]+p[3]))+((p[4]+p[5])+(p[6]+p[7]))
            X[t]=acc-s
    return out

def factor(g, rank):
    row=lax.broadcasted_iota(jnp.int32,(128,128),0); col=lax.broadcasted_iota(jnp.int32,(128,128),1)
    keep=(row<rank)&(col<rank)
    masked=jnp.where(keep,g,0.0)
    eye=row==col
    trace=jnp.sum(jnp.where(eye,masked,0.0),keepdims=True)
    delta=0.01*trace/jnp.full((1,1),rank,jnp.int32).astype(F)
    a=masked*(1.0/delta)+jnp.where(eye,1.0,0.0)
    linv=jnp.concatenate(eliminate([a[8*t:8*t+8] for t in range(16)]),axis=0)
    linv=jnp.where(keep,linv*lax.rsqrt(delta),0.0)
    return masked, linv

def dot(a, b):
    return jnp.dot(a, b, precision=HIGHEST, preferred_element_type=F)


def dot_tn(a, b):
    return lax.dot_general(a, b, (((0,), (0,)), ((), ())), precision=HIGHEST, preferred_element_type=F)


def dot_nt(a, b):
    return lax.dot_general(a, b, (((1,), (1,)), ((), ())), precision=HIGHEST, preferred_element_type=F)


def leaf_kernel(rank_ref, gram_ref, weights_ref, zeta_ref, h_ref):
    masked, linv = factor(gram_ref[...], rank_ref[0])
    weights_ref[...] = linv.T.astype(jnp.bfloat16)
    zeta = dot(linv, masked)
    zeta_ref[...] = zeta
    h_ref[...] = dot_tn(zeta, zeta)


def merge_kernel(rank_ref, own_ref, partner_ref, child_ref, moved_ref, zeta_ref, h_ref):
    masked, linv = factor((own_ref[...] + partner_ref[...]) * 0.5, rank_ref[0])
    moved_ref[...] = dot_nt(child_ref[...], linv)
    zeta = dot(linv, masked)
    zeta_ref[...] = zeta
    h_ref[...] = dot_tn(zeta, zeta)


def square(dtype=F):
    return jax.ShapeDtypeStruct((128, 128), dtype)


def specs(count):
    return [pl.BlockSpec(memory_space=pltpu.SMEM)] + [pl.BlockSpec(memory_space=pltpu.VMEM)] * count


def climb_level(child_z, own_gram, partner_gram, rank):
    return pl.pallas_call(
        merge_kernel, out_shape=(square(), square(), square()), in_specs=specs(3)
    )(rank, own_gram, partner_gram, child_z)


def local(probes, filter_taps, cluster_ranks):
    combined = composite(filter_taps)
    reach = (combined.shape[1] - 1) // 2
    rows, cols, width = probes.shape
    tall = extended(probes, (("tx", 0),), reach)
    middle = jnp.dot(
        toeplitz(combined[0], rows),
        tall.reshape(tall.shape[0], cols * width),
        preferred_element_type=jnp.float32,
    )
    middle = middle.reshape(rows, cols, width).astype(jnp.bfloat16)
    broad = extended(middle, (("ty", 1),), reach)
    sketch = jnp.einsum(
        "yc,xcp->xyp", toeplitz(combined[1], cols), broad, preferred_element_type=jnp.float32
    ).astype(jnp.bfloat16)
    flat = sketch.reshape(rows * cols, width)
    gram = jnp.einsum("np,nq->pq", flat, flat, preferred_element_type=jnp.float32) / (rows * cols)
    row_at = lax.axis_index("tx")
    col_at = lax.axis_index("ty")
    rank = cluster_ranks[0, row_at, col_at].reshape(1)
    weights, zeta, grams = pl.pallas_call(
        leaf_kernel, out_shape=(square(jnp.bfloat16), square(), square()), in_specs=specs(1)
    )(rank, gram)
    leaf_basis = (
        jnp.dot(flat, weights, preferred_element_type=jnp.float32)
        .astype(jnp.bfloat16)
        .reshape(rows, cols, width)
    )
    row_two = row_at - row_at % 2
    row_four = row_at - row_at % 4
    col_two = col_at - col_at % 2
    col_four = col_at - col_at % 4
    partner = from_partner(grams, "tx", 0)
    first_e, zeta, grams = climb_level(
        zeta, grams, partner, cluster_ranks[1, row_two, col_at].reshape(1)
    )
    partner = from_partner(grams, "ty", 0)
    second_e, zeta, grams = climb_level(
        zeta, grams, partner, cluster_ranks[2, row_two, col_two].reshape(1)
    )
    partner = from_partner(grams, "tx", 1)
    third_e, zeta, grams = climb_level(
        zeta, grams, partner, cluster_ranks[3, row_four, col_two].reshape(1)
    )
    partner = from_partner(grams, "ty", 1)
    fourth_e, zeta, grams = climb_level(
        zeta, grams, partner, cluster_ranks[4, row_four, col_four].reshape(1)
    )
    transfers = jnp.stack([first_e, second_e, third_e, fourth_e], axis=0)[None, None]
    return (leaf_basis, transfers)


def solution(mesh):
    in_specs = (P("tx", "ty", None), P(), P())
    out_specs = (P("tx", "ty", None), P("tx", "ty", None, None, None))
    return jax.shard_map(local, mesh=mesh, in_specs=in_specs, out_specs=out_specs, check_vma=False)
```

time: 313 us -> 218 us (0.70)
  other arithmetic: 137 us -> 10.3 us
  Pallas kernels: 0 us -> 37.6 us
  local copies, waits for them, and re-layouts: 24.5 us -> 15.8 us
  starting transfers between devices: 33.8 us -> 41.5 us
  between operations: 8.26 us -> 1.16 us
  waiting for transfers between devices: 65.1 us -> 71.3 us
  matrix products: 39 us -> 35.8 us
    another operation x25 -> x0, other arithmetic: 114 us -> none  [the longest x15 61.9 us: factor(): return (masked, jnp.linalg.cholesky(shifted))]
    pallas_call x0 -> x5, Pallas kernels: none -> 37.6 us  [the longest x4 30.1 us: climb_level(): pl.pallas_call(merge_kernel, out_shape=(square(), square(), square()), in...]
    ppermute x4, starting transfers between devices: 21.4 us -> 29.2 us  [from_partner(): lax.ppermute(shard, axis, [(i, i ^ 1 << stride) for i in range(lax.axis_s...]
    gather x5 -> x0, local copies, waits for them, and re-layouts: 7.74 us -> none  [factor(): trace_sum = jnp.sum(jnp.diagonal(masked, axis1=-2, axis2=-1), axis=-1)]
    sub x5 -> x0, other arithmetic: 5.71 us -> none  [factor(): 1.0 - keep_mask]
    ppermute x4, waiting for transfers between devices: 5.68 us -> 10.7 us  [from_partner(): lax.ppermute(shard, axis, [(i, i ^ 1 << stride) for i in range(lax.axis_s...]
    reduce_sum x6 -> x0, other arithmetic: 4.29 us -> none  [the longest x5 3.01 us: factor(): trace_sum = jnp.sum(jnp.diagonal(masked, axis1=-2, axis2=-1), axis=-1)]
    convert_element_type x5 -> x0, other arithmetic: 3.19 us -> none  [rank_mask(): return (jnp.arange(width) < rank_value[..., None]).astype(jnp.float32)]
  transfers between devices with their start and end apart: 8 -> 8, of which waited for: 5 -> 6; matrix products, arithmetic and copies ran while one was open for 6% -> 4% of each run, Pallas kernels for 0% -> 0%
where the time goes in v1:
time: 218 us; the launch traced here: 213 us
  waiting for transfers between devices  71.3 us (33%)
  starting transfers between devices  41.5 us (19%)
  Pallas kernels  37.6 us (17%)
  matrix products  35.8 us (16%)
  local copies, waits for them, and re-layouts  15.8 us (7%)
  other arithmetic  10.3 us (5%)
    ppermute x2, waiting for transfers between devices, extended(): lax.ppermute(lax.slice_in_dim(block, 0, width, axis=dim), axis, backward)  53.2 us
    pallas_call x4, Pallas kernels, climb_level(): pl.pallas_call(merge_kernel, out_shape=(square(), square(), square()), in...  30.1 us
    ppermute x4, starting transfers between devices, from_partner(): lax.ppermute(shard, axis, [(i, i ^ 1 << stride) for i in range(lax.axis_s...  29.2 us
    dot_general x1, matrix products, local(): jnp.dot(toeplitz(combined[0], rows), tall.reshape(tall.shape[0], cols * w...  21.2 us
    slice x2, local copies, waits for them, and re-layouts, extended(): lax.slice_in_dim(block, block.shape[dim] - width, None, axis=dim)  10.7 us
    ppermute x4, waiting for transfers between devices, from_partner(): lax.ppermute(shard, axis, [(i, i ^ 1 << stride) for i in range(lax.axis_s...  10.7 us
    concatenate x2, other arithmetic, extended(): block = jnp.concatenate([low, block, high], axis=dim)  8.71 us
    pallas_call x1, Pallas kernels, local(): pl.pallas_call(leaf_kernel, out_shape=(square(jnp.bfloat16), square(), sq...  7.48 us
  transfers between devices with their start and end apart: 8, of which 6 were waited for; matrix products, arithmetic and copies ran while one was open for 4% of the time, Pallas kernels for 0%

profile of v1, /device:TPU:96, one launch (start us, length us, event | category | flops | bytes accessed | tf_op | source)
XLA Modules:
  0.0 213.4 jit_solution(3918203357273249776)
XLA Ops:
  0.6 7.0 %fusion.29 = (bf16[80,128,128]{2,1,0:T(8,128)(2,1)}, bf16[80,128,128]{2,1,0:T(8,128)(2,1)}) fusion(bf16[128,128,128]{2,1,0:T(8,128)(2,1)} %param.3), kind=kLoop, calls=%fused_computation.36 | loop fusion | bytes 10485760 | tf_op jit(solution)/shard_map/slice | solution.py:18
  7.7 4.5 %collective-permute-start.1 = (bf16[80,128,128]{2,1,0:T(8,128)(2,1)}, bf16[80,128,128]{2,1,0:T(8,128)(2,1)S(1)}, u32[]{:S(2)}, u32[]{:S(2)}) collective-permute-start(bf16[80,128,128]{2,1,0:T(8,128)(2,1)} %get-tuple-element.33), channel_id=1, source_target_pairs={{8,0},{16,8},{24,16},{32,24},{40,32},{48,40},{56,48},{64,56},{72,6... | collective-permute-start | bytes 7864328 | tf_op jit(solution)/shard_map/ppermute | solution.py:20
  12.1 1.9 collective-permute-start
  15.3 53.2 %collective-permute-done.1 = bf16[80,128,128]{2,1,0:T(8,128)(2,1)S(1)} collective-permute-done((bf16[80,128,128]{2,1,0:T(8,128)(2,1)}, bf16[80,128,128]{2,1,0:T(8,128)(2,1)S(1)}, u32[]{:S(2)}, u32[]{:S(2)}) %collective-permute-start.1) | collective-permute-done | bytes 2621472 | tf_op jit(solution)/shard_map/ppermute | solution.py:20
  68.5 6.2 %collective-permute-done = bf16[80,128,128]{2,1,0:T(8,128)(2,1)} collective-permute-done((bf16[80,128,128]{2,1,0:T(8,128)(2,1)}, bf16[80,128,128]{2,1,0:T(8,128)(2,1)}, u32[]{:S(2)}, u32[]{:S(2)}) %collective-permute-start) | collective-permute-done | bytes 2621472 | tf_op jit(solution)/shard_map/ppermute | solution.py:17
  74.8 4.6 %pad_maximum_fusion = bf16[288,128,128]{2,1,0:T(8,128)(2,1)S(1)} fusion(bf16[80,128,128]{2,1,0:T(8,128)(2,1)S(1)} %collective-permute-done.1, bf16[128,128,128]{2,1,0:T(8,128)(2,1)} %param.3, bf16[80,128,128]{2,1,0:T(8,128)(2,1)} %collective-permute-done), kind=kLoop, calls=%fused_computation.5 | loop fusion | flops 9437184 | bytes 18874368 | tf_op jit(solution)/shard_map/concatenate | solution.py:21
  79.4 21.2 %fusion.10 = bf16[128,128,128]{2,0,1:T(8,128)(2,1)S(1)} fusion(bf16[128,288]{1,0:T(8,128)(2,1)S(1)} %reshape.52, bf16[36,8,128,128]{3,2,1,0:T(8,128)(2,1)S(1)} %bitcast.54), kind=kOutput, calls=%fused_computation.12 | convolution fusion | flops 1210056704 | bytes 13705216 | tf_op jit(solution)/shard_map/dot_general | solution.py:142
  100.6 3.7 %fusion.28 = (bf16[128,80,128]{2,0,1:T(8,128)(2,1)}, bf16[128,80,128]{2,0,1:T(8,128)(2,1)}) fusion(bf16[128,128,128]{2,0,1:T(8,128)(2,1)S(1)} %fusion.10), kind=kLoop, calls=%fused_computation.35 | loop fusion | bytes 10485760 | tf_op jit(solution)/shard_map/slice | solution.py:18
  104.3 1.3 collective-permute-start.3
  105.6 4.7 %collective-permute-start.2 = (bf16[128,80,128]{2,0,1:T(8,128)(2,1)}, bf16[128,80,128]{2,0,1:T(8,128)(2,1)}, u32[]{:S(2)}, u32[]{:S(2)}) collective-permute-start(bf16[128,80,128]{2,0,1:T(8,128)(2,1)} %get-tuple-element.30), channel_id=1, source_target_pairs={{0,1},{1,2},{2,3},{3,4},{4,5},{5,6},{6,7},{8,9},{9,10},{10,11},{11... | collective-permute-start | bytes 7864328 | tf_op jit(solution)/shard_map/ppermute | solution.py:17
  110.8 1.4 constant_dynamic-slice_fusion.2
  112.3 1.2 collective-permute-done.2
  113.5 4.1 %pad_maximum_fusion.1 = bf16[128,288,128]{2,0,1:T(8,128)(2,1)S(1)} fusion(bf16[128,80,128]{2,0,1:T(8,128)(2,1)S(1)} %collective-permute-done.3, bf16[128,128,128]{2,0,1:T(8,128)(2,1)} %copy-done, bf16[128,80,128]{2,0,1:T(8,128)(2,1)} %collective-permute-done.2), kind=kLoop, calls=%fused_computation.6 | loop fusion | flops 9437184 | bytes 18874368 | tf_op jit(solution)/shard_map/concatenate | solution.py:21
  117.6 6.5 %fusion.7 = bf16[128,128,128]{1,2,0:T(8,128)(2,1)S(1)} fusion(bf16[128,288,128]{2,0,1:T(8,128)(2,1)S(1)} %pad_maximum_fusion.1, bf16[128,288]{1,0:T(8,128)(2,1)S(1)} %reshape.54), kind=kOutput, calls=%fused_computation.11 | convolution fusion | flops 1210056704 | bytes 13705216 | tf_op jit(solution)/shard_map/yc,xcp->xyp/dot_general | solution.py:149
  124.1 2.0 fusion.17.gram_ref
  126.1 7.5 %shard_map.50 = (bf16[128,128]{1,0:T(8,128)(2,1)}, f32[128,128]{1,0:T(8,128)}, f32[128,128]{1,0:T(8,128)}) custom-call(s32[1]{0:T(128)} %bitcast.8.rank_ref, f32[128,128]{1,0:T(8,128)} %fusion.17.gram_ref), custom_call_target="tpu_custom_call" | custom-call | tf_op jit(solution)/shard_map/pallas_call | solution.py:157
  133.8 4.5 %collective-permute-done.4.partner_ref = f32[128,128]{1,0:T(8,128)S(1)} collective-permute-done((f32[128,128]{1,0:T(8,128)}, f32[128,128]{1,0:T(8,128)S(1)}, u32[]{:S(2)}, u32[]{:S(2)}) %collective-permute-start.4) | collective-permute-done | bytes 65568 | tf_op jit(solution)/shard_map/ppermute | solution.py:26
  138.2 0.6 copy-done.3
  138.9 7.5 %shard_map.51 = (f32[128,128]{1,0:T(8,128)}, f32[128,128]{1,0:T(8,128)}, f32[128,128]{1,0:T(8,128)}) custom-call(s32[1]{0:T(128)} %bitcast.11.rank_ref, f32[128,128]{1,0:T(8,128)} %get-tuple-element.16.own_ref, f32[128,128]{1,0:T(8,128)} %copy-done.3, f32[128,128]{1,0:T(8,128)} %get-tuple-element.17.child_ref), custom_call_target="tpu_custom_call" | custom-call | tf_op jit(solution)/shard_map/pallas_call | solution.py:132
  146.4 24.0 %collective-permute-start.5 = (f32[128,128]{1,0:T(8,128)}, f32[128,128]{1,0:T(8,128)S(1)}, u32[]{:S(2)}, u32[]{:S(2)}) collective-permute-start(f32[128,128]{1,0:T(8,128)} %get-tuple-element.19.own_ref), channel_id=1, source_target_pairs={{0,1},{1,0},{2,3},{3,2},{4,5},{5,4},{6,7},{7,6},{8,9},{9,8},{10,11... | collective-permute-start | bytes 196616 | tf_op jit(solution)/shard_map/ppermute | solution.py:26
  170.4 1.1 collective-permute-done.5.partner_ref
  171.5 0.6 copy-done.4
  172.2 7.6 %shard_map.52 = (f32[128,128]{1,0:T(8,128)}, f32[128,128]{1,0:T(8,128)}, f32[128,128]{1,0:T(8,128)}) custom-call(s32[1]{0:T(128)} %bitcast.13.rank_ref, f32[128,128]{1,0:T(8,128)} %get-tuple-element.19.own_ref, f32[128,128]{1,0:T(8,128)} %copy-done.4, f32[128,128]{1,0:T(8,128)} %get-tuple-element.20.child_ref), custom_call_target="tpu_custom_call" | custom-call | tf_op jit(solution)/shard_map/pallas_call | solution.py:132
  179.8 1.0 collective-permute-start.6
  180.7 5.1 %collective-permute-done.6.partner_ref = f32[128,128]{1,0:T(8,128)S(1)} collective-permute-done((f32[128,128]{1,0:T(8,128)}, f32[128,128]{1,0:T(8,128)S(1)}, u32[]{:S(2)}, u32[]{:S(2)}) %collective-permute-start.6) | collective-permute-done | bytes 65568 | tf_op jit(solution)/shard_map/ppermute | solution.py:26
  185.8 0.6 copy-done.5
  186.5 7.5 %shard_map.53 = (f32[128,128]{1,0:T(8,128)}, f32[128,128]{1,0:T(8,128)}, f32[128,128]{1,0:T(8,128)}) custom-call(s32[1]{0:T(128)} %bitcast.15.rank_ref, f32[128,128]{1,0:T(8,128)} %get-tuple-element.22.own_ref, f32[128,128]{1,0:T(8,128)} %copy-done.5, f32[128,128]{1,0:T(8,128)} %get-tuple-element.23.child_ref), custom_call_target="tpu_custom_call" | custom-call | tf_op jit(solution)/shard_map/pallas_call | solution.py:132
  194.0 4.0 %collective-permute-start.7 = (f32[128,128]{1,0:T(8,128)}, f32[128,128]{1,0:T(8,128)S(1)}, u32[]{:S(2)}, u32[]{:S(2)}) collective-permute-start(f32[128,128]{1,0:T(8,128)} %get-tuple-element.25.own_ref), channel_id=1, source_target_pairs={{0,2},{1,3},{2,0},{3,1},{4,6},{5,7},{6,4},{7,5},{8,10},{9,11},{10,... | collective-permute-start | bytes 196616 | tf_op jit(solution)/shard_map/ppermute | solution.py:26
  198.0 5.5 %convolution_convert_fusion = bf16[16384,128]{1,0:T(8,128)(2,1)} fusion(bf16[16384,128]{1,0:T(8,128)(2,1)} %bitcast.55, bf16[128,128]{1,0:T(8,128)(2,1)} %get-tuple-element.15), kind=kOutput, calls=%fused_computation | convolution fusion | flops 538968064 | bytes 8421376 | tf_op jit(solution)/shard_map/dot_general | solution.py:161
  203.5 0.6 copy-done.2
  204.1 7.5 %shard_map.54 = (f32[128,128]{1,0:T(8,128)}, f32[128,128]{1,0:T(8,128)}, f32[128,128]{1,0:T(8,128)}) custom-call(s32[1]{0:T(128)} %bitcast.17.rank_ref, f32[128,128]{1,0:T(8,128)} %get-tuple-element.25.own_ref, f32[128,128]{1,0:T(8,128)} %copy-done.2, f32[128,128]{1,0:T(8,128)} %get-tuple-element.26.child_ref), custom_call_target="tpu_custom_call" | custom-call | tf_op jit(solution)/shard_map/pallas_call | solution.py:132
  211.6 1.6 maximum_bitcast_fusion
  (35 shorter events, 2.0 us)
Async XLA Ops:
  0.6 13.4 %copy-start.9 = (f32[2,2,33]{2,1,0:T(2,128)S(1)}, f32[2,2,33]{2,1,0:T(2,128)}, u32[]{:S(2)}) copy-start(f32[2,2,33]{2,1,0:T(2,128)} %param.4) | copy-start | bytes 1588
  7.7 60.9 %collective-permute-start.1 = (bf16[80,128,128]{2,1,0:T(8,128)(2,1)}, bf16[80,128,128]{2,1,0:T(8,128)(2,1)S(1)}, u32[]{:S(2)}, u32[]{:S(2)}) collective-permute-start(bf16[80,128,128]{2,1,0:T(8,128)(2,1)} %get-tuple-element.33), channel_id=1, source_target_pairs={{8,0},{16,8},{24,16},{32,24},{40,32},{48,40},{56,48},{64,56},{72,6... | collective-permute-start | bytes 7864328 | tf_op jit(solution)/shard_map/ppermute | solution.py:20
  12.1 62.6 %collective-permute-start = (bf16[80,128,128]{2,1,0:T(8,128)(2,1)}, bf16[80,128,128]{2,1,0:T(8,128)(2,1)}, u32[]{:S(2)}, u32[]{:S(2)}) collective-permute-start(bf16[80,128,128]{2,1,0:T(8,128)(2,1)} %get-tuple-element.32), channel_id=1, source_target_pairs={{0,8},{8,16},{16,24},{24,32},{32,40},{40,48},{48,56},{56,64},{64,7... | collective-permute-start | bytes 7864328 | tf_op jit(solution)/shard_map/ppermute | solution.py:17
  100.6 3.7 %copy-start = (bf16[128,128,128]{2,0,1:T(8,128)(2,1)}, bf16[128,128,128]{2,0,1:T(8,128)(2,1)S(1)}, u32[]{:S(2)}) copy-start(bf16[128,128,128]{2,0,1:T(8,128)(2,1)S(1)} %fusion.10) | copy-start | bytes 12582916
  104.3 8.0 %collective-permute-start.3 = (bf16[128,80,128]{2,0,1:T(8,128)(2,1)}, bf16[128,80,128]{2,0,1:T(8,128)(2,1)S(1)}, u32[]{:S(2)}, u32[]{:S(2)}) collective-permute-start(bf16[128,80,128]{2,0,1:T(8,128)(2,1)} %get-tuple-element.31), channel_id=1, source_target_pairs={{1,0},{2,1},{3,2},{4,3},{5,4},{6,5},{7,6},{9,8},{10,9},{11,10},{12... | collective-permute-start | bytes 7864328 | tf_op jit(solution)/shard_map/ppermute | solution.py:20
  105.6 7.9 %collective-permute-start.2 = (bf16[128,80,128]{2,0,1:T(8,128)(2,1)}, bf16[128,80,128]{2,0,1:T(8,128)(2,1)}, u32[]{:S(2)}, u32[]{:S(2)}) collective-permute-start(bf16[128,80,128]{2,0,1:T(8,128)(2,1)} %get-tuple-element.30), channel_id=1, source_target_pairs={{0,1},{1,2},{2,3},{3,4},{4,5},{5,6},{6,7},{8,9},{9,10},{10,11},{11... | collective-permute-start | bytes 7864328 | tf_op jit(solution)/shard_map/ppermute | solution.py:17
  124.1 2.0 copy-start.1
  133.6 4.7 %collective-permute-start.4 = (f32[128,128]{1,0:T(8,128)}, f32[128,128]{1,0:T(8,128)S(1)}, u32[]{:S(2)}, u32[]{:S(2)}) collective-permute-start(f32[128,128]{1,0:T(8,128)} %get-tuple-element.16.own_ref), channel_id=1, source_target_pairs={{0,8},{8,0},{16,24},{24,16},{32,40},{40,32},{48,56},{56,48},{64,72... | collective-permute-start | bytes 196616 | tf_op jit(solution)/shard_map/ppermute | solution.py:26
  138.2 0.6 copy-start.3
  146.4 25.1 %collective-permute-start.5 = (f32[128,128]{1,0:T(8,128)}, f32[128,128]{1,0:T(8,128)S(1)}, u32[]{:S(2)}, u32[]{:S(2)}) collective-permute-start(f32[128,128]{1,0:T(8,128)} %get-tuple-element.19.own_ref), channel_id=1, source_target_pairs={{0,1},{1,0},{2,3},{3,2},{4,5},{5,4},{6,7},{7,6},{8,9},{9,8},{10,11... | collective-permute-start | bytes 196616 | tf_op jit(solution)/shard_map/ppermute | solution.py:26
  171.5 0.6 copy-start.4
  179.8 6.1 %collective-permute-start.6 = (f32[128,128]{1,0:T(8,128)}, f32[128,128]{1,0:T(8,128)S(1)}, u32[]{:S(2)}, u32[]{:S(2)}) collective-permute-start(f32[128,128]{1,0:T(8,128)} %get-tuple-element.22.own_ref), channel_id=1, source_target_pairs={{0,16},{8,24},{16,0},{24,8},{32,48},{40,56},{48,32},{56,40},{64,80... | collective-permute-start | bytes 196616 | tf_op jit(solution)/shard_map/ppermute | solution.py:26
  185.8 0.6 copy-start.5
  194.0 9.5 %collective-permute-start.7 = (f32[128,128]{1,0:T(8,128)}, f32[128,128]{1,0:T(8,128)S(1)}, u32[]{:S(2)}, u32[]{:S(2)}) collective-permute-start(f32[128,128]{1,0:T(8,128)} %get-tuple-element.25.own_ref), channel_id=1, source_target_pairs={{0,2},{1,3},{2,0},{3,1},{4,6},{5,7},{6,4},{7,5},{8,10},{9,11},{10,... | collective-permute-start | bytes 196616 | tf_op jit(solution)/shard_map/ppermute | solution.py:26
  198.0 13.6 %copy-start.6 = (f32[128,128]{1,0:T(8,128)S(1)}, f32[128,128]{1,0:T(8,128)}, u32[]{:S(2)}) copy-start(f32[128,128]{1,0:T(8,128)} %get-tuple-element.18) | copy-start | bytes 196612
  198.0 13.6 %copy-start.7 = (f32[128,128]{1,0:T(8,128)S(1)}, f32[128,128]{1,0:T(8,128)}, u32[]{:S(2)}) copy-start(f32[128,128]{1,0:T(8,128)} %get-tuple-element.21) | copy-start | bytes 196612
  198.0 13.6 %copy-start.8 = (f32[128,128]{1,0:T(8,128)S(1)}, f32[128,128]{1,0:T(8,128)}, u32[]{:S(2)}) copy-start(f32[128,128]{1,0:T(8,128)} %get-tuple-element.24) | copy-start | bytes 196612
  203.5 0.6 copy-start.2

commit v2 on v1

v2 whole, which is shorter than its diff:
```python
import jax
import jax.numpy as jnp
from jax import lax
from jax.experimental import pallas as pl
from jax.experimental.pallas import tpu as pltpu
from jax.sharding import PartitionSpec as P

HIGHEST = lax.Precision.HIGHEST
F = jnp.float32


def composite(filter_taps):
    count = filter_taps.shape[-1]
    wide = 5 * (count - 1) + 1
    first = jnp.arange(count)[:, None, None]
    second = jnp.arange(count)[None, :, None]
    spot = jnp.arange(wide)[None, None, :]
    table = (first + 4 * second == spot).astype(jnp.float32)
    outer = filter_taps[:, 0, :, None] * filter_taps[:, 1, None, :]
    return jnp.einsum("dab,abm->dm", outer, table, precision=lax.Precision.HIGHEST).astype(
        jnp.bfloat16
    )


def lane_of(x, i): return jnp.broadcast_to(x[:, i:i+1], (8,128))
def row_of(x, i): return jnp.broadcast_to(x[i:i+1,:], (8,128))

def eliminate(X):
    sub=lax.broadcasted_iota(jnp.int32,(8,128),0); lane=lax.broadcasted_iota(jnp.int32,(8,128),1)
    X=list(X); out=[]
    for b in range(16):
        j=8*b
        head=X[b]
        B=[lane_of(head,j+c) for c in range(8)]
        C={t:[lane_of(X[t],j+c) for c in range(8)] for t in range(b+1,16)}
        inblk=(lane>=j)&(lane<j+8)
        head=jnp.where(inblk,jnp.where(lane-j==sub,1.0,0.0),head)
        V=jnp.zeros((8,128),F)
        for c in range(8):
            d=row_of(B[c],c)
            inv=1.0/d
            prow=row_of(head,c)
            V=jnp.where(sub==c,prow*lax.rsqrt(d),V)
            prow=prow*inv
            col=B[c]
            head=jnp.where(sub==c,prow,head-col*prow)
            for e in range(c+1,8):
                brow=row_of(B[e],c)*inv
                B[e]=jnp.where(sub==c,brow,B[e]-col*brow)
        out.append(jnp.where(lane<=j+sub,V,0.0))
        rows=[row_of(head,c) for c in range(8)]
        for t in range(b+1,16):
            acc=jnp.where(inblk,0.0,X[t])
            p=[C[t][c]*rows[c] for c in range(8)]
            s=((p[0]+p[1])+(p[2]+p[3]))+((p[4]+p[5])+(p[6]+p[7]))
            X[t]=acc-s
    return out

def factor(g, rank):
    row=lax.broadcasted_iota(jnp.int32,(128,128),0); col=lax.broadcasted_iota(jnp.int32,(128,128),1)
    keep=(row<rank)&(col<rank)
    masked=jnp.where(keep,g,0.0)
    eye=row==col
    trace=jnp.sum(jnp.where(eye,masked,0.0),keepdims=True)
    delta=0.01*trace/jnp.full((1,1),rank,jnp.int32).astype(F)
    a=masked*(1.0/delta)+jnp.where(eye,1.0,0.0)
    linv=jnp.concatenate(eliminate([a[8*t:8*t+8] for t in range(16)]),axis=0)
    linv=jnp.where(keep,linv*lax.rsqrt(delta),0.0)
    return masked, linv

def dot(a, b):
    return jnp.dot(a, b, precision=HIGHEST, preferred_element_type=F)


def dot_tn(a, b):
    return lax.dot_general(a, b, (((0,), (0,)), ((), ())), precision=HIGHEST, preferred_element_type=F)


def dot_nt(a, b):
    return lax.dot_general(a, b, (((1,), (1,)), ((), ())), precision=HIGHEST, preferred_element_type=F)


MESH = pl.DeviceIdType.MESH


def partner_of(level, row_at, col_at):
    step = (level + 1) // 2
    odd = level % 2
    row = row_at + odd * step * (1 - 2 * ((row_at // step) % 2))
    col = col_at + (1 - odd) * step * (1 - 2 * ((col_at // step) % 2))
    return row, col


def tree_kernel(
    ranks, gram_ref, weights_ref, moved_ref, own, other, zeta_ref, send_sem, recv_sem
):
    row_at, col_at = lax.axis_index("tx"), lax.axis_index("ty")
    barrier = pltpu.get_barrier_semaphore()

    @pl.loop(1, 5)
    def _(level):
        pl.semaphore_signal(
            barrier, inc=1, device_id=partner_of(level, row_at, col_at), device_id_type=MESH
        )

    def swap(level):
        return pltpu.make_async_remote_copy(
            src_ref=own.at[level],
            dst_ref=other.at[level],
            send_sem=send_sem.at[level],
            recv_sem=recv_sem.at[level],
            device_id=partner_of(level, row_at, col_at),
            device_id_type=MESH,
        )

    masked, linv = factor(gram_ref[...], ranks[0, row_at, col_at])
    zeta = dot(linv, masked)
    zeta_ref[...] = zeta
    own[1] = dot_tn(zeta, zeta)
    pl.semaphore_wait(barrier, 4)
    swap(1).start()
    weights_ref[...] = linv.T.astype(jnp.bfloat16)

    @pl.loop(1, 5)
    def _(level):
        span_x = jnp.where(level < 3, 2, 4)
        span_y = jnp.where(level < 2, 1, jnp.where(level < 4, 2, 4))
        rank = ranks[level, row_at - row_at % span_x, col_at - col_at % span_y]
        swap(level).wait_recv()
        masked, linv = factor((own[level] + other[level]) * 0.5, rank)
        child = zeta_ref[...]

        @pl.when(level < 4)
        def _():
            zeta = dot(linv, masked)
            zeta_ref[...] = zeta
            own[level + 1] = dot_tn(zeta, zeta)
            swap(level + 1).start()

        moved_ref[0, 0, level - 1] = dot_nt(child, linv)

    @pl.loop(1, 5)
    def _(level):
        swap(level).wait_send()


def tree(ranks, gram):
    return pl.pallas_call(
        tree_kernel,
        out_shape=(
            jax.ShapeDtypeStruct((128, 128), jnp.bfloat16),
            jax.ShapeDtypeStruct((1, 1, 4, 128, 128), F),
        ),
        in_specs=[
            pl.BlockSpec(memory_space=pltpu.SMEM),
            pl.BlockSpec(memory_space=pltpu.VMEM),
        ],
        out_specs=(
            pl.BlockSpec(memory_space=pltpu.VMEM),
            pl.BlockSpec(memory_space=pltpu.VMEM),
        ),
        scratch_shapes=[
            pltpu.VMEM((5, 128, 128), F),
            pltpu.VMEM((5, 128, 128), F),
            pltpu.VMEM((128, 128), F),
            pltpu.SemaphoreType.DMA((5,)),
            pltpu.SemaphoreType.DMA((5,)),
        ],
        compiler_params=pltpu.CompilerParams(collective_id=1, has_side_effects=True),
        name="tree",
    )(ranks, gram)


def basis_kernel(flat_ref, weights_ref, out_ref):
    out_ref[...] = jnp.dot(
        flat_ref[...], weights_ref[...], preferred_element_type=F
    ).astype(jnp.bfloat16)


def basis(flat, weights):
    rows = 2048
    return pl.pallas_call(
        basis_kernel,
        grid=(flat.shape[0] // rows,),
        out_shape=jax.ShapeDtypeStruct(flat.shape, jnp.bfloat16),
        in_specs=[
            pl.BlockSpec((rows, 128), lambda i: (i, 0)),
            pl.BlockSpec((128, 128), lambda i: (0, 0)),
        ],
        out_specs=pl.BlockSpec((rows, 128), lambda i: (i, 0)),
        name="basis",
    )(flat, weights)


REACH = 80
SIDE = 128
STEPS = 8


def stretched(line, length, width):
    sub = lax.broadcasted_iota(jnp.int32, (8, width), 0)
    base = jnp.broadcast_to(line, (8, width))
    for bit in (1, 2, 4):
        base = jnp.where((sub // bit) % 2 == 1, pltpu.roll(base, bit, 1), base)
    tiles = [base] + [pltpu.roll(base, 8 * t, 1) for t in range(1, length // 8)]
    return jnp.concatenate(tiles, axis=0)


def halo_kernel(
    lines_x, lines_y, probes, sketch, gram_ref, tall, broad, out_slots, mix, across,
    own_sem, out_sem, row_send, row_recv, col_send, col_recv,
):
    n_x, n_y = lax.axis_size("tx"), lax.axis_size("ty")
    row_at, col_at = lax.axis_index("tx"), lax.axis_index("ty")
    has_up, has_down = row_at > 0, row_at < n_x - 1
    has_left, has_right = col_at > 0, col_at < n_y - 1
    up, down = (row_at - 1, col_at), (row_at + 1, col_at)
    left, right = (row_at, col_at - 1), (row_at, col_at + 1)
    sides = ((has_up, up), (has_down, down), (has_left, left), (has_right, right))

    load = pltpu.make_async_copy(probes, tall.at[pl.ds(REACH, SIDE)], own_sem)
    load.start()
    barrier = pltpu.get_barrier_semaphore()
    for there, device in sides:
        @pl.when(there)
        def _():
            pl.semaphore_signal(barrier, inc=1, device_id=device, device_id_type=MESH)
    peers = [there.astype(jnp.int32) for there, _ in sides]
    pl.semaphore_wait(barrier, peers[0] + peers[1] + peers[2] + peers[3])

    def row_copy(to_down, step, first):
        count = 24 if first else 8
        far = 8 * step + 24
        if to_down:
            source, target, device, way = SIDE - far, REACH - far, down, 0
        else:
            source, target, device, way = far - count, REACH + SIDE + far - count, up, 1
        return pltpu.make_async_remote_copy(
            src_ref=probes.at[pl.ds(source, count)],
            dst_ref=tall.at[pl.ds(target, count)],
            send_sem=row_send.at[way, step],
            recv_sem=row_recv.at[way, step],
            device_id=device,
            device_id_type=MESH,
        )

    def col_copy(to_right, step, low):
        rows = 8 * (7 - step) if low else 8 * (8 + step)
        if to_right:
            source, target, device, way = SIDE, 0, right, 0
        else:
            source, target, device, way = REACH, REACH + SIDE, left, 1
        half = 0 if low else 1
        return pltpu.make_async_remote_copy(
            src_ref=broad.at[pl.ds(rows, 8), pl.ds(source, REACH)],
            dst_ref=broad.at[pl.ds(rows, 8), pl.ds(target, REACH)],
            send_sem=col_send.at[way, half, step],
            recv_sem=col_recv.at[way, half, step],
            device_id=device,
            device_id_type=MESH,
        )

    def each(action, step, first=False):
        for there, to_down in ((has_down, True), (has_up, False)):
            @pl.when(there)
            def _():
                action(row_copy(to_down, step, first))

    def each_arrival(step, first=False):
        for there, to_down in ((has_up, True), (has_down, False)):
            @pl.when(there)
            def _():
                row_copy(to_down, step, first).wait_recv()

    start = lambda copy: copy.start()
    sent = lambda copy: copy.wait_send()
    each(start, 0, True)
    each(start, 1)
    mix[...] = stretched(lines_x[...], 128, mix.shape[1]).astype(jnp.bfloat16)
    across[...] = stretched(lines_y[...], 128, across.shape[1]).astype(jnp.bfloat16)

    @pl.when(jnp.logical_not(has_up))
    def _():
        tall[pl.ds(0, REACH)] = jnp.zeros((REACH, SIDE, SIDE), jnp.bfloat16)

    @pl.when(jnp.logical_not(has_down))
    def _():
        tall[pl.ds(REACH + SIDE, REACH)] = jnp.zeros((REACH, SIDE, SIDE), jnp.bfloat16)

    @pl.when(jnp.logical_not(has_left))
    def _():
        broad[:, pl.ds(0, REACH)] = jnp.zeros((SIDE, REACH, SIDE), jnp.bfloat16)

    @pl.when(jnp.logical_not(has_right))
    def _():
        broad[:, pl.ds(REACH + SIDE, REACH)] = jnp.zeros((SIDE, REACH, SIDE), jnp.bfloat16)

    gram_ref[...] = jnp.zeros_like(gram_ref)
    load.wait()

    def filter_rows(step):
        @pl.loop(0, 8)
        def _(index):
            block = index // 4
            rows = pl.multiple_of(8 * (7 - step + block * (1 + 2 * step)), 8)
            cols = pl.multiple_of(32 * (index % 4), 32)
            depth = 8 + 2 * REACH
            pair = [
                tall[pl.ds(rows, depth), pl.ds(cols + 16 * k, 16)].reshape(depth * 16, SIDE)
                for k in range(2)
            ]
            middle = jnp.dot(
                mix[...], jnp.concatenate(pair, axis=1), preferred_element_type=F
            ).astype(jnp.bfloat16)
            for k in range(2):
                broad[pl.ds(rows, 8), pl.ds(REACH + cols + 16 * k, 16)] = middle[
                    :, SIDE * k : SIDE * (k + 1)
                ].reshape(8, 16, SIDE)

    def out_copy(step, half):
        rows = 8 * (7 - step) if half == 0 else 8 * (8 + step)
        return pltpu.make_async_copy(
            out_slots.at[step, pl.ds(8 * half, 8)], sketch.at[pl.ds(rows, 8)], out_sem.at[step, half]
        )

    def send_cols(step):
        for there, to_right in ((has_right, True), (has_left, False)):
            for low in (True, False):
                @pl.when(there)
                def _():
                    col_copy(to_right, step, low).start()

    def filter_cols(step):
        for there, to_right in ((has_left, True), (has_right, False)):
            for low in (True, False):
                @pl.when(there)
                def _():
                    col_copy(to_right, step, low).wait_recv()

        @pl.loop(0, 8)
        def _(index):
            block = index // 4
            rows = 8 * (7 - step + block * (1 + 2 * step)) + 2 * (index % 4)
            pair = [broad[rows + k] for k in range(2)]
            result = jnp.dot(
                across[:, : SIDE + 2 * REACH],
                jnp.concatenate(pair, axis=1),
                preferred_element_type=F,
            ).astype(jnp.bfloat16)
            slot = 2 * index
            for k in range(2):
                out_slots[step, slot + k] = result[:, SIDE * k : SIDE * (k + 1)]

        flat = out_slots[step].reshape(16 * SIDE, SIDE)
        gram_ref[...] += lax.dot_general(
            flat, flat, (((0,), (0,)), ((), ())), preferred_element_type=F
        )
        for half in range(2):
            out_copy(step, half).start()

    each_arrival(0, True)
    filter_rows(0)
    send_cols(0)
    each(sent, 0, True)
    each(start, 2)

    @pl.loop(1, STEPS)
    def _(step):
        each_arrival(step)
        filter_rows(step)
        send_cols(step)
        each(sent, step)

        @pl.when(step < STEPS - 2)
        def _():
            each(start, step + 2)
        filter_cols(step - 1)

    filter_cols(STEPS - 1)

    @pl.loop(0, STEPS)
    def _(step):
        for half in range(2):
            out_copy(step, half).wait()
        for there, to_right in ((has_right, True), (has_left, False)):
            for low in (True, False):
                @pl.when(there)
                def _():
                    col_copy(to_right, step, low).wait_send()

    gram_ref[...] = gram_ref[...] * (1.0 / (SIDE * SIDE))


def halo(lines_x, lines_y, probes):
    bf = jnp.bfloat16
    return pl.pallas_call(
        halo_kernel,
        out_shape=(
            jax.ShapeDtypeStruct((SIDE, SIDE, SIDE), bf),
            jax.ShapeDtypeStruct((SIDE, SIDE), F),
        ),
        in_specs=[
            pl.BlockSpec(memory_space=pltpu.VMEM),
            pl.BlockSpec(memory_space=pltpu.VMEM),
            pl.BlockSpec(memory_space=pl.ANY),
        ],
        out_specs=(
            pl.BlockSpec(memory_space=pl.ANY),
            pl.BlockSpec(memory_space=pltpu.VMEM),
        ),
        scratch_shapes=[
            pltpu.VMEM((SIDE + 2 * REACH, SIDE, SIDE), bf),
            pltpu.VMEM((SIDE, SIDE + 2 * REACH, SIDE), bf),
            pltpu.VMEM((STEPS, 16, SIDE, SIDE), bf),
            pltpu.VMEM((SIDE, 16 * (8 + 2 * REACH)), bf),
            pltpu.VMEM((SIDE, 384), bf),
            pltpu.SemaphoreType.DMA,
            pltpu.SemaphoreType.DMA((STEPS, 2)),
            pltpu.SemaphoreType.DMA((2, STEPS)),
            pltpu.SemaphoreType.DMA((2, STEPS)),
            pltpu.SemaphoreType.DMA((2, 2, STEPS)),
            pltpu.SemaphoreType.DMA((2, 2, STEPS)),
        ],
        compiler_params=pltpu.CompilerParams(
            collective_id=0, has_side_effects=True, vmem_limit_bytes=50 * 2**20
        ),
        name="halo",
    )(lines_x, lines_y, probes)


def local(probes, filter_taps, cluster_ranks):
    combined = composite(filter_taps).astype(F)
    wide = combined.shape[1]
    lines_x = jnp.pad(combined[0][:, None], ((0, 168 - wide), (0, 15))).reshape(1, 168 * 16)
    lines_y = jnp.pad(combined[1][None], ((0, 0), (0, 384 - wide)))
    sketch, gram = halo(lines_x, lines_y, probes)
    weights, transfers = tree(cluster_ranks, gram)
    leaf_basis = basis(sketch.reshape(SIDE * SIDE, SIDE), weights).reshape(probes.shape)
    return (leaf_basis, transfers)


def solution(mesh):
    in_specs = (P("tx", "ty", None), P(), P())
    out_specs = (P("tx", "ty", None), P("tx", "ty", None, None, None))
    return jax.shard_map(local, mesh=mesh, in_specs=in_specs, out_specs=out_specs, check_vma=False)
```

time: 218 us -> 133 us (0.61); the launches traced: 213 us -> 133 us
  Pallas kernels: 37.6 us -> 128 us
  waiting for transfers between devices: 71.3 us -> 0 us
  starting transfers between devices: 41.5 us -> 0 us
  matrix products: 35.8 us -> 0.62 us
  local copies, waits for them, and re-layouts: 15.8 us -> 3.89 us
  other arithmetic: 10.3 us -> 0.01 us
    pallas_call x5 -> x3, Pallas kernels: 37.6 us -> 128 us  [the longest x1 72.5 us: halo(): pl.pallas_call(halo_kernel, out_shape=(jax.ShapeDtypeStruct((SIDE, SIDE,...]
    ppermute x8 -> x0, waiting for transfers between devices: 71.3 us -> none  [the longest x2 53.2 us: extended(): lax.ppermute(lax.slice_in_dim(block, 0, width, axis=dim), axis, backward)]
    ppermute x8 -> x0, starting transfers between devices: 41.5 us -> none  [the longest x4 29.2 us: from_partner(): lax.ppermute(shard, axis, [(i, i ^ 1 << stride) for i in range(lax.axis_s...]
    dot_general x4 -> x0, matrix products: 35.1 us -> none  [the longest x1 21.2 us: local(): jnp.dot(toeplitz(combined[0], rows), tall.reshape(tall.shape[0], cols * w...]
    slice x5 -> x1, local copies, waits for them, and re-layouts: 10.8 us -> 0.01 us  [local(): lines_y = jnp.pad(combined[1][None], ((0, 0), (0, 384 - wide)))]
    concatenate x2 -> x0, other arithmetic: 8.71 us -> none  [extended(): block = jnp.concatenate([low, block, high], axis=dim)]
  transfers between devices with their start and end apart: 8 -> 0, of which waited for: 6 -> 0; matrix products, arithmetic and copies ran while one was open for 4% -> 0% of each run, Pallas kernels for 0% -> 0%
where the time goes in v2:
time: 133 us
  Pallas kernels  128 us (96%)
  local copies, waits for them, and re-layouts  3.89 us (3%)
    pallas_call x1, Pallas kernels, halo(): pl.pallas_call(halo_kernel, out_shape=(jax.ShapeDtypeStruct((SIDE, SIDE,...  72.5 us
    pallas_call x1, Pallas kernels, tree(): pl.pallas_call(tree_kernel, out_shape=(jax.ShapeDtypeStruct((128, 128), j...  47.8 us
    pallas_call x1, Pallas kernels, basis(): pl.pallas_call(basis_kernel, grid=(flat.shape[0] // rows,), out_shape=jax...  7.5 us
    unnamed x7, local copies, waits for them, and re-layouts  2.9 us

profile of v2, /device:TPU:96, one launch (start us, length us, event | category | flops | bytes accessed | tf_op | source)
XLA Modules:
  0.0 133.0 jit_solution(16907599571406943609)
XLA Ops:
  0.6 0.8 fusion.9
  1.4 0.1 copy.7
  1.5 0.6 fusion.3
  2.2 1.5 %copy.9.ranks = s32[5,32,8]{2,1,0:T(8,128)} copy(s32[5,32,8]{1,2,0:T(8,128)} %param.5) | data formatting | bytes 10240 | tf_op args[2]
  3.6 0.1 copy.10
  3.7 0.1 reshape.42.lines_x
  3.9 72.5 %halo.1 = (bf16[128,128,128]{2,1,0:T(8,128)(2,1)}, f32[128,128]{1,0:T(8,128)S(1)}) custom-call(f32[1,2688]{1,0:T(1,128)S(1)} %reshape.42.lines_x, f32[1,384]{1,0:T(1,128)S(1)} %pad.9.lines_y, bf16[128,128,128]{2,1,0:T(8,128)(2,1)} %probes.1), custom_call_target="tpu_custom_call" | custom-call | tf_op jit(solution)/shard_map/halo/pallas_call | solution.py:396
  76.4 0.0 copy-start
  76.4 0.6 copy-done
  77.0 47.8 %tree.1 = (bf16[128,128]{1,0:T(8,128)(2,1)}, f32[1,1,4,128,128]{4,3,2,1,0:T(8,128)}) custom-call(s32[5,32,8]{2,1,0:T(8,128)} %copy.9.ranks, f32[128,128]{1,0:T(8,128)} %copy-done), custom_call_target="tpu_custom_call" | custom-call | tf_op jit(solution)/shard_map/tree/pallas_call | solution.py:148
  124.8 0.0 copy-start.1
  124.8 7.5 %basis.1 = bf16[16384,128]{1,0:T(8,128)(2,1)} custom-call(bf16[16384,128]{1,0:T(8,128)(2,1)} %bitcast.12, bf16[128,128]{1,0:T(8,128)(2,1)} %get-tuple-element.8.weights_ref), custom_call_target="tpu_custom_call" | custom-call | tf_op jit(solution)/shard_map/basis/pallas_call | solution.py:182
  132.3 0.0 copy-done.1
  132.3 0.7 copy.12
  (5 shorter events, 0.0 us)
Async XLA Ops:
  76.4 0.6 copy-start
  124.8 7.5 %copy-start.1 = (f32[1,1,4,128,128]{4,3,2,1,0:T(8,128)S(1)}, f32[1,1,4,128,128]{4,3,2,1,0:T(8,128)}, u32[]{:S(2)}) copy-start(f32[1,1,4,128,128]{4,3,2,1,0:T(8,128)} %get-tuple-element.17) | copy-start | bytes 786436

commit v3 on v2

v3 whole, which is shorter than its diff:
```python
import jax
import jax.numpy as jnp
from jax import lax
from jax.experimental import pallas as pl
from jax.experimental.pallas import tpu as pltpu
from jax.sharding import PartitionSpec as P

HIGHEST = lax.Precision.HIGHEST
F = jnp.float32
BF = jnp.bfloat16
REACH = 80
SIDE = 128
STEPS = 8
MESH = pl.DeviceIdType.MESH


def lane_of(x, i):
    return jnp.broadcast_to(x[:, i : i + 1], (8, 128))


def row_of(x, i):
    return jnp.broadcast_to(x[i : i + 1, :], (8, 128))


def split(a):
    one = a.astype(BF)
    rest = a - one.astype(F)
    two = rest.astype(BF)
    return one, two, (rest - two.astype(F)).astype(BF)


def eliminate(tiles):
    sub = lax.broadcasted_iota(jnp.int32, (8, 128), 0)
    lane = lax.broadcasted_iota(jnp.int32, (8, 128), 1)
    tiles, out = list(tiles), []
    for b in range(8):
        j = 16 * b
        rows = [tiles[2 * b], tiles[2 * b + 1]]
        cols = [[lane_of(rows[h], j + c) for c in range(16)] for h in range(2)]
        near = range(2 * b + 2, min(2 * b + 4, 16))
        below = {t: [lane_of(tiles[t], j + c) for c in range(16)] for t in near}
        a1, a2, a3 = split(jnp.concatenate(rows, axis=0))
        inside = (lane >= j) & (lane < j + 16)
        rows = [
            jnp.where(inside, jnp.where(lane - j == sub + 8 * h, 1.0, 0.0), rows[h]) for h in range(2)
        ]
        kept = [jnp.zeros((8, 128), F) for _ in range(2)]
        for c in range(16):
            h, s = divmod(c, 8)
            pivot = row_of(cols[h][c], s)
            inv = 1.0 / pivot
            line = row_of(rows[h], s)
            kept[h] = jnp.where(sub == s, line * lax.rsqrt(pivot), kept[h])
            line = line * inv
            for g in range(2):
                new = rows[g] - cols[g][c] * line
                rows[g] = jnp.where(sub == s, line, new) if g == h else new
            for e in range(c + 1, 16):
                line_e = row_of(cols[h][e], s) * inv
                for g in range(2):
                    new = cols[g][e] - cols[g][c] * line_e
                    cols[g][e] = jnp.where(sub == s, line_e, new) if g == h else new
        out += [jnp.where(lane <= j + 8 * h + sub, kept[h], 0.0) for h in range(2)]
        lines = [row_of(rows[c // 8], c % 8) for c in range(16)]
        for t in near:
            terms = [below[t][c] * lines[c] for c in range(16)]
            while len(terms) > 1:
                terms = [terms[i] + terms[i + 1] for i in range(0, len(terms), 2)]
            tiles[t] = jnp.where(inside, 0.0, tiles[t]) - terms[0]
        if b < 6:
            b1, b2, b3 = split(jnp.concatenate(rows, axis=0))
            change = lax.dot_general(
                jnp.concatenate([a1, a1, a2, a2, a1, a3], axis=0),
                jnp.concatenate([b1, b2, b1, b2, b3, b1], axis=0),
                (((0,), (0,)), ((), ())),
                preferred_element_type=F,
            )
            for t in range(2 * b + 4, 16):
                tiles[t] = jnp.where(inside, 0.0, tiles[t]) - change[8 * t : 8 * t + 8]
    return out


def factor(g, rank):
    row=lax.broadcasted_iota(jnp.int32,(128,128),0); col=lax.broadcasted_iota(jnp.int32,(128,128),1)
    keep=(row.astype(F)<rank)&(col.astype(F)<rank)
    masked=jnp.where(keep,g,0.0)
    eye=row==col
    trace=jnp.sum(jnp.where(eye,masked,0.0),keepdims=True)
    delta=0.01*trace/rank
    a=masked*(1.0/delta)+jnp.where(eye,1.0,0.0)
    linv=jnp.concatenate(eliminate([a[8*t:8*t+8] for t in range(16)]),axis=0)
    linv=jnp.where(keep,linv*lax.rsqrt(delta),0.0)
    return masked, linv

def dot(a, b):
    return jnp.dot(a, b, precision=HIGHEST, preferred_element_type=F)


def dot_tn(a, b):
    return lax.dot_general(a, b, (((0,), (0,)), ((), ())), precision=HIGHEST, preferred_element_type=F)


def dot_nt(a, b):
    return lax.dot_general(a, b, (((1,), (1,)), ((), ())), precision=HIGHEST, preferred_element_type=F)


def partner_of(level, row_at, col_at):
    step = (level + 1) // 2
    odd = level % 2
    row = row_at + odd * step * (1 - 2 * ((row_at // step) % 2))
    col = col_at + (1 - odd) * step * (1 - 2 * ((col_at // step) % 2))
    return row, col


def combine(taps, pads):
    pads[...] = jnp.zeros_like(pads)
    for which in range(2):
        for dim in range(2):
            pads[which, dim : dim + 1, 0 : taps.shape[2]] = taps[dim, which : which + 1, :]
    first, second = pads[0], pads[1]
    total = jnp.zeros_like(first)
    for b in range(taps.shape[2]):
        moved = pltpu.roll(first, 4 * b, 1) if b else first
        total = total + moved * jnp.broadcast_to(second[:, b : b + 1], first.shape)
    return total.astype(BF)

def stretched(line, length, width):
    sub = lax.broadcasted_iota(jnp.int32, (8, width), 0)
    base = jnp.broadcast_to(line, (8, width))
    for bit in (1, 2, 4):
        base = jnp.where((sub // bit) % 2 == 1, pltpu.roll(base, bit, 1), base)
    tiles = [base] + [pltpu.roll(base, 8 * t, 1) for t in range(1, length // 8)]
    return jnp.concatenate(tiles, axis=0)


def body(
    taps, ranks, probes, sketch, weights_ref, moved_ref,
    tall, broad, out_slots, mix, across, part, gram_ref, taps_ref, ranks_ref, pads, own, other, zeta_ref,
    small_sem, own_sem, out_sem, row_send, row_recv, col_send, col_recv, swap_send, swap_recv,
):
    n_x, n_y = lax.axis_size("tx"), lax.axis_size("ty")
    row_at, col_at = lax.axis_index("tx"), lax.axis_index("ty")
    has_up, has_down = row_at > 0, row_at < n_x - 1
    has_left, has_right = col_at > 0, col_at < n_y - 1
    up, down = (row_at - 1, col_at), (row_at + 1, col_at)
    left, right = (row_at, col_at - 1), (row_at, col_at + 1)
    sides = ((has_up, up), (has_down, down), (has_left, left), (has_right, right))

    load = pltpu.make_async_copy(probes, tall.at[pl.ds(REACH, SIDE)], own_sem)
    load.start()
    small = [
        pltpu.make_async_copy(taps, taps_ref, small_sem.at[0]),
        pltpu.make_async_copy(ranks, ranks_ref, small_sem.at[1]),
    ]
    for copy in small:
        copy.start()
    barrier = pltpu.get_barrier_semaphore()
    for there, device in sides:
        @pl.when(there)
        def _():
            pl.semaphore_signal(barrier, inc=1, device_id=device, device_id_type=MESH)

    @pl.loop(1, 5)
    def _(level):
        pl.semaphore_signal(
            barrier, inc=1, device_id=partner_of(level, row_at, col_at), device_id_type=MESH
        )

    peers = [there.astype(jnp.int32) for there, _ in sides]
    pl.semaphore_wait(barrier, peers[0] + peers[1] + peers[2] + peers[3] + 4)

    def row_copy(to_down, step, first):
        count = 24 if first else 8
        far = 8 * step + 24
        if to_down:
            source, target, device, way = SIDE - far, REACH - far, down, 0
        else:
            source, target, device, way = far - count, REACH + SIDE + far - count, up, 1
        return pltpu.make_async_remote_copy(
            src_ref=probes.at[pl.ds(source, count)],
            dst_ref=tall.at[pl.ds(target, count)],
            send_sem=row_send.at[way, step],
            recv_sem=row_recv.at[way, step],
            device_id=device,
            device_id_type=MESH,
        )

    def col_copy(to_right, step, low):
        rows = 8 * (7 - step) if low else 8 * (8 + step)
        if to_right:
            source, target, device, way = SIDE, 0, right, 0
        else:
            source, target, device, way = REACH, REACH + SIDE, left, 1
        half = 0 if low else 1
        return pltpu.make_async_remote_copy(
            src_ref=broad.at[pl.ds(rows, 8), pl.ds(source, REACH)],
            dst_ref=broad.at[pl.ds(rows, 8), pl.ds(target, REACH)],
            send_sem=col_send.at[way, half, step],
            recv_sem=col_recv.at[way, half, step],
            device_id=device,
            device_id_type=MESH,
        )

    def each(action, step, first=False):
        for there, to_down in ((has_down, True), (has_up, False)):
            @pl.when(there)
            def _():
                action(row_copy(to_down, step, first))

    def each_arrival(step, first=False):
        for there, to_down in ((has_up, True), (has_down, False)):
            @pl.when(there)
            def _():
                row_copy(to_down, step, first).wait_recv()

    start = lambda copy: copy.start()
    sent = lambda copy: copy.wait_send()
    each(start, 0, True)
    each(start, 1)
    for copy in small:
        copy.wait()
    lines = combine(taps_ref, pads)
    wide = mix.shape[1]
    spot = lax.broadcasted_iota(jnp.int32, (256, wide), 1)
    spread = jnp.where(spot == 16 * lax.broadcasted_iota(jnp.int32, (256, wide), 0), 1.0, 0.0)
    line_x = jnp.dot(lines, spread.astype(BF), preferred_element_type=F)[0:1]
    line_y = jnp.concatenate([lines[1:2].astype(F), jnp.zeros((1, 128), F)], axis=1)
    mix[...] = stretched(line_x, 128, wide).astype(BF)
    across[...] = stretched(line_y, 128, across.shape[1]).astype(BF)

    @pl.when(jnp.logical_not(has_up))
    def _():
        tall[pl.ds(0, REACH)] = jnp.zeros((REACH, SIDE, SIDE), BF)

    @pl.when(jnp.logical_not(has_down))
    def _():
        tall[pl.ds(REACH + SIDE, REACH)] = jnp.zeros((REACH, SIDE, SIDE), BF)

    @pl.when(jnp.logical_not(has_left))
    def _():
        broad[:, pl.ds(0, REACH)] = jnp.zeros((SIDE, REACH, SIDE), BF)

    @pl.when(jnp.logical_not(has_right))
    def _():
        broad[:, pl.ds(REACH + SIDE, REACH)] = jnp.zeros((SIDE, REACH, SIDE), BF)

    gram_ref[...] = jnp.zeros_like(gram_ref)
    load.wait()

    def place(step, index):
        block = index // 4
        rows = pl.multiple_of(8 * (7 - step + block * (1 + 2 * step)), 8)
        return block, rows, pl.multiple_of(32 * (index % 4), 32)

    def columns(rows, depth, cols):
        return jnp.concatenate(
            [
                tall[pl.ds(rows, depth), pl.ds(cols + 16 * k, 16)].reshape(depth * 16, SIDE)
                for k in range(2)
            ],
            axis=1,
        )

    def begin_rows(step):
        @pl.loop(0, 8)
        def _(index):
            block, rows, cols = place(step, index)
            near = 8 * (1 - block)
            weight = mix[:, pl.ds(pl.multiple_of(16 * near, 128), 32 * REACH)]
            part[index] = jnp.dot(
                weight, columns(rows + near, 2 * REACH, cols), preferred_element_type=F
            )

    def finish_rows(step):
        @pl.loop(0, 8)
        def _(index):
            block, rows, cols = place(step, index)
            far = 2 * REACH * block
            weight = mix[:, pl.ds(pl.multiple_of(16 * far, 128), 128)]
            middle = (
                part[index]
                + jnp.dot(weight, columns(rows + far, 8, cols), preferred_element_type=F)
            ).astype(BF)
            for k in range(2):
                broad[pl.ds(rows, 8), pl.ds(REACH + cols + 16 * k, 16)] = middle[
                    :, SIDE * k : SIDE * (k + 1)
                ].reshape(8, 16, SIDE)

    def out_copy(step, half):
        rows = 8 * (7 - step) if half == 0 else 8 * (8 + step)
        return pltpu.make_async_copy(
            out_slots.at[step, pl.ds(8 * half, 8)], sketch.at[pl.ds(rows, 8)], out_sem.at[step, half]
        )

    def send_cols(step):
        for there, to_right in ((has_right, True), (has_left, False)):
            for low in (True, False):
                @pl.when(there)
                def _():
                    col_copy(to_right, step, low).start()

    def filter_cols(step):
        for there, to_right in ((has_left, True), (has_right, False)):
            for low in (True, False):
                @pl.when(there)
                def _():
                    col_copy(to_right, step, low).wait_recv()

        @pl.loop(0, 8)
        def _(index):
            block = index // 4
            rows = 8 * (7 - step + block * (1 + 2 * step)) + 2 * (index % 4)
            pair = [broad[rows + k] for k in range(2)]
            result = jnp.dot(
                across[:, : SIDE + 2 * REACH],
                jnp.concatenate(pair, axis=1),
                preferred_element_type=F,
            ).astype(BF)
            slot = 2 * index
            for k in range(2):
                out_slots[step, slot + k] = result[:, SIDE * k : SIDE * (k + 1)]

        flat = out_slots[step].reshape(16 * SIDE, SIDE)
        gram_ref[...] += lax.dot_general(
            flat, flat, (((0,), (0,)), ((), ())), preferred_element_type=F
        )
        for half in range(2):
            out_copy(step, half).start()

    each_arrival(0, True)
    begin_rows(0)

    @pl.loop(0, STEPS)
    def _(step):
        @pl.when(step > 0)
        def _():
            each_arrival(step)
        finish_rows(step)
        send_cols(step)

        @pl.when(step == 0)
        def _():
            each(sent, 0, True)

        @pl.when(step > 0)
        def _():
            each(sent, step)

        @pl.when(step < STEPS - 2)
        def _():
            each(start, step + 2)

        @pl.when(step < STEPS - 1)
        def _():
            begin_rows(step + 1)

        @pl.when(step > 0)
        def _():
            filter_cols(step - 1)

    filter_cols(STEPS - 1)

    def swap(level):
        return pltpu.make_async_remote_copy(
            src_ref=own.at[level],
            dst_ref=other.at[level],
            send_sem=swap_send.at[level],
            recv_sem=swap_recv.at[level],
            device_id=partner_of(level, row_at, col_at),
            device_id_type=MESH,
        )

    def rank_at(level, row, col):
        table = ranks_ref[level]
        spot = (lax.broadcasted_iota(jnp.int32, table.shape, 0) == col) & (
            lax.broadcasted_iota(jnp.int32, table.shape, 1) == row
        )
        return jnp.sum(jnp.where(spot, table, 0).astype(F), keepdims=True)

    masked, linv = factor(gram_ref[...] * (1.0 / (SIDE * SIDE)), rank_at(0, row_at, col_at))
    zeta = dot(linv, masked)
    zeta_ref[...] = zeta
    own[1] = dot_tn(zeta, zeta)
    swap(1).start()
    weights_ref[...] = linv.T.astype(BF)

    @pl.loop(1, 5)
    def _(level):
        span_x = jnp.where(level < 3, 2, 4)
        span_y = jnp.where(level < 2, 1, jnp.where(level < 4, 2, 4))
        rank = rank_at(level, row_at - row_at % span_x, col_at - col_at % span_y)
        swap(level).wait_recv()
        masked, linv = factor((own[level] + other[level]) * 0.5, rank)
        child = zeta_ref[...]

        @pl.when(level < 4)
        def _():
            zeta = dot(linv, masked)
            zeta_ref[...] = zeta
            own[level + 1] = dot_tn(zeta, zeta)
            swap(level + 1).start()

        moved_ref[0, 0, level - 1] = dot_nt(child, linv)

    @pl.loop(1, 5)
    def _(level):
        swap(level).wait_send()

    @pl.loop(0, STEPS)
    def _(step):
        for half in range(2):
            out_copy(step, half).wait()
        for there, to_right in ((has_right, True), (has_left, False)):
            for low in (True, False):
                @pl.when(there)
                def _():
                    col_copy(to_right, step, low).wait_send()


def compress(taps, ranks, probes):
    depth = 8 + 2 * REACH
    return pl.pallas_call(
        body,
        out_shape=(
            jax.ShapeDtypeStruct((SIDE, SIDE, SIDE), BF),
            jax.ShapeDtypeStruct((SIDE, SIDE), BF),
            jax.ShapeDtypeStruct((1, 1, 4, SIDE, SIDE), F),
        ),
        in_specs=[pl.BlockSpec(memory_space=pl.ANY)] * 3,
        out_specs=(
            pl.BlockSpec(memory_space=pl.ANY),
            pl.BlockSpec(memory_space=pltpu.VMEM),
            pl.BlockSpec(memory_space=pltpu.VMEM),
        ),
        scratch_shapes=[
            pltpu.VMEM((SIDE + 2 * REACH, SIDE, SIDE), BF),
            pltpu.VMEM((SIDE, SIDE + 2 * REACH, SIDE), BF),
            pltpu.VMEM((STEPS, 16, SIDE, SIDE), BF),
            pltpu.VMEM((SIDE, 16 * depth), BF),
            pltpu.VMEM((SIDE, 384), BF),
            pltpu.VMEM((8, SIDE, 2 * SIDE), F),
            pltpu.VMEM((SIDE, SIDE), F),
            pltpu.VMEM(taps.shape, F),
            pltpu.VMEM(ranks.shape, jnp.int32),
            pltpu.VMEM((2, 16, 256), F),
            pltpu.VMEM((5, SIDE, SIDE), F),
            pltpu.VMEM((5, SIDE, SIDE), F),
            pltpu.VMEM((SIDE, SIDE), F),
            pltpu.SemaphoreType.DMA((2,)),
            pltpu.SemaphoreType.DMA,
            pltpu.SemaphoreType.DMA((STEPS, 2)),
            pltpu.SemaphoreType.DMA((2, STEPS)),
            pltpu.SemaphoreType.DMA((2, STEPS)),
            pltpu.SemaphoreType.DMA((2, 2, STEPS)),
            pltpu.SemaphoreType.DMA((2, 2, STEPS)),
            pltpu.SemaphoreType.DMA((5,)),
            pltpu.SemaphoreType.DMA((5,)),
        ],
        compiler_params=pltpu.CompilerParams(
            collective_id=0, has_side_effects=True, vmem_limit_bytes=50 * 2**20
        ),
        name="compress",
    )(taps, ranks, probes)


CHUNKS = 8


def basis_kernel(sketch, weights_ref, moved, out, moved_out, source, result, load_sem, store_sem, pass_sem):
    rows = SIDE // CHUNKS

    def part(ref, index):
        return ref.at[pl.ds(rows * index, rows)]

    def load(index):
        return pltpu.make_async_copy(part(sketch, index), part(source, index), load_sem.at[index])

    def store(index):
        return pltpu.make_async_copy(part(result, index), part(out, index), store_sem.at[index])

    for index in range(CHUNKS):
        load(index).start()
    forward = pltpu.make_async_copy(moved, moved_out, pass_sem)
    forward.start()
    weights = weights_ref[...]
    zero = jnp.zeros_like(weights)
    twice = jnp.concatenate(
        [jnp.concatenate([weights, zero], axis=1), jnp.concatenate([zero, weights], axis=1)], axis=0
    )

    @pl.loop(0, CHUNKS)
    def _(index):
        load(index).wait()
        half = rows // 2
        base = rows * index
        pair = [
            source[pl.ds(base + half * k, half)].reshape(half * SIDE, SIDE) for k in range(2)
        ]
        both = jnp.dot(jnp.concatenate(pair, axis=1), twice, preferred_element_type=F).astype(BF)
        for k in range(2):
            result[pl.ds(base + half * k, half)] = both[:, SIDE * k : SIDE * (k + 1)].reshape(
                half, SIDE, SIDE
            )
        store(index).start()

    for index in range(CHUNKS):
        store(index).wait()
    forward.wait()


def basis(sketch, weights, moved):
    anywhere = pl.BlockSpec(memory_space=pl.ANY)
    return pl.pallas_call(
        basis_kernel,
        out_shape=(
            jax.ShapeDtypeStruct(sketch.shape, BF),
            jax.ShapeDtypeStruct(moved.shape, F),
        ),
        in_specs=[anywhere, pl.BlockSpec(memory_space=pltpu.VMEM), anywhere],
        out_specs=(anywhere, anywhere),
        scratch_shapes=[
            pltpu.VMEM(sketch.shape, BF),
            pltpu.VMEM(sketch.shape, BF),
            pltpu.SemaphoreType.DMA((CHUNKS,)),
            pltpu.SemaphoreType.DMA((CHUNKS,)),
            pltpu.SemaphoreType.DMA,
        ],
        compiler_params=pltpu.CompilerParams(vmem_limit_bytes=24 * 2**20),
        name="basis",
    )(sketch, weights, moved)


def local(probes, filter_taps, cluster_ranks):
    sketch, weights, moved = compress(filter_taps, jnp.swapaxes(cluster_ranks, 1, 2), probes)
    return basis(sketch, weights, moved)


def solution(mesh):
    in_specs = (P("tx", "ty", None), P(), P())
    out_specs = (P("tx", "ty", None), P("tx", "ty", None, None, None))
    return jax.shard_map(local, mesh=mesh, in_specs=in_specs, out_specs=out_specs, check_vma=False)
```

time: 133 us -> 118 us (0.89)
  Pallas kernels: 128 us -> 114 us
    pallas_call x3 -> x2, Pallas kernels: 128 us -> 114 us  [the longest x1 110 us: compress(): pl.pallas_call(body, out_shape=(jax.ShapeDtypeStruct((SIDE, SIDE, SIDE),...]
    unnamed x7 -> x6, local copies, waits for them, and re-layouts: 2.9 us -> 3.58 us
where the time goes in v3:
time: 118 us
  Pallas kernels  114 us (97%)
  local copies, waits for them, and re-layouts  3.58 us (3%)
    pallas_call x1, Pallas kernels, compress(): pl.pallas_call(body, out_shape=(jax.ShapeDtypeStruct((SIDE, SIDE, SIDE),...  110 us
    pallas_call x1, Pallas kernels, basis(): pl.pallas_call(basis_kernel, out_shape=(jax.ShapeDtypeStruct(sketch.shape...  3.64 us
    unnamed x6, local copies, waits for them, and re-layouts  3.58 us

profile of v3, /device:TPU:96, one launch (start us, length us, event | category | flops | bytes accessed | tf_op | source)
XLA Modules:
  0.0 117.8 jit_solution(8297958832447858219)
XLA Ops:
  0.6 0.0 copy-start.1
  0.6 0.7 copy-done.1
  1.4 0.0 copy-start.2
  1.4 0.7 copy-done.2
  2.0 109.9 %compress.1 = (bf16[128,128,128]{2,1,0:T(8,128)(2,1)}, bf16[128,128]{1,0:T(8,128)(2,1)S(1)}, f32[1,1,4,128,128]{4,3,2,1,0:T(8,128)S(1)}) custom-call(f32[2,2,33]{2,1,0:T(2,128)S(1)} %copy-done.2, s32[5,8,32]{2,1,0:T(8,128)S(1)} %bitcast.1, bf16[128,128,128]{2,1,0:T(8,128)(2,1)} %probes.1), custom_call_target="tpu_custom_call" | custom-call | tf_op jit(solution)/shard_map/compress/pallas_call | solution.py:422
  112.0 0.0 copy-start
  112.0 2.2 %copy-done = bf16[128,128,128]{2,1,0:T(8,128)(2,1)S(1)} copy-done((bf16[128,128,128]{2,1,0:T(8,128)(2,1)S(1)}, bf16[128,128,128]{2,1,0:T(8,128)(2,1)}, u32[]{:S(2)}) %copy-start) | copy-done | bytes 4194328
  114.2 3.6 %basis.1 = (bf16[128,128,128]{2,1,0:T(8,128)(2,1)}, f32[1,1,4,128,128]{4,3,2,1,0:T(8,128)}) custom-call(bf16[128,128,128]{2,1,0:T(8,128)(2,1)S(1)} %copy-done, bf16[128,128]{1,0:T(8,128)(2,1)S(1)} %get-tuple-element.6.weights_ref, f32[1,1,4,128,128]{4,3,2,1,0:T(8,128)S(1)} %get-tuple-element.7.moved), custom_call_target="tpu_custom_call" | custom-call | tf_op jit(solution)/shard_map/basis/pallas_call | solution.py:513
Async XLA Ops:
  0.6 0.7 copy-start.1
  1.4 0.7 copy-start.2
  112.0 2.2 %copy-start = (bf16[128,128,128]{2,1,0:T(8,128)(2,1)S(1)}, bf16[128,128,128]{2,1,0:T(8,128)(2,1)}, u32[]{:S(2)}) copy-start(bf16[128,128,128]{2,1,0:T(8,128)(2,1)} %get-tuple-element.5.sketch) | copy-start | bytes 12582916

commit v4 on v3

--- a/solution.py
+++ b/solution.py
@@ -135,8 +135,8 @@
 
 def body(
     taps, ranks, probes, sketch, weights_ref, moved_ref,
-    tall, broad, out_slots, mix, across, part, gram_ref, taps_ref, ranks_ref, pads, own, other, zeta_ref,
-    small_sem, own_sem, out_sem, row_send, row_recv, col_send, col_recv, swap_send, swap_recv,
+    tall, broad, mix, across, part, gram_ref, taps_ref, ranks_ref, pads, own, other, zeta_ref,
+    small_sem, own_sem, row_send, row_recv, col_send, col_recv, swap_send, swap_recv,
 ):
     n_x, n_y = lax.axis_size("tx"), lax.axis_size("ty")
     row_at, col_at = lax.axis_index("tx"), lax.axis_index("ty")
@@ -247,50 +247,49 @@
     gram_ref[...] = jnp.zeros_like(gram_ref)
     load.wait()
 
-    def place(step, index):
-        block = index // 4
-        rows = pl.multiple_of(8 * (7 - step + block * (1 + 2 * step)), 8)
-        return block, rows, pl.multiple_of(32 * (index % 4), 32)
+    def first_row(step, block):
+        return pl.multiple_of(8 * (7 - step + block * (1 + 2 * step)), 8)
+
+    def place(step, block, group):
+        return 4 * block + group, first_row(step, block), 32 * group
+
+    def aligned(cols):
+        return cols if isinstance(cols, int) else pl.multiple_of(cols, 16)
 
     def columns(rows, depth, cols):
         return jnp.concatenate(
             [
-                tall[pl.ds(rows, depth), pl.ds(cols + 16 * k, 16)].reshape(depth * 16, SIDE)
+                tall[pl.ds(rows, depth), pl.ds(aligned(cols + 16 * k), 16)].reshape(depth * 16, SIDE)
                 for k in range(2)
             ],
             axis=1,
         )
 
     def begin_rows(step):
-        @pl.loop(0, 8)
-        def _(index):
-            block, rows, cols = place(step, index)
-            near = 8 * (1 - block)
-            weight = mix[:, pl.ds(pl.multiple_of(16 * near, 128), 32 * REACH)]
-            part[index] = jnp.dot(
-                weight, columns(rows + near, 2 * REACH, cols), preferred_element_type=F
-            )
+        @pl.loop(0, 4)
+        def _(group):
+            for block in range(2):
+                index, rows, cols = place(step, block, group)
+                near = 8 * (1 - block)
+                part[index] = jnp.dot(
+                    mix[:, 16 * near : 16 * near + 32 * REACH],
+                    columns(rows + near, 2 * REACH, cols),
+                    preferred_element_type=F,
+                )
 
     def finish_rows(step):
-        @pl.loop(0, 8)
-        def _(index):
-            block, rows, cols = place(step, index)
+        for block, group in [(block, group) for block in range(2) for group in range(4)]:
+            index, rows, cols = place(step, block, group)
             far = 2 * REACH * block
-            weight = mix[:, pl.ds(pl.multiple_of(16 * far, 128), 128)]
+            newest = columns(rows + far, 8, cols)
             middle = (
                 part[index]
-                + jnp.dot(weight, columns(rows + far, 8, cols), preferred_element_type=F)
+                + jnp.dot(mix[:, 16 * far : 16 * far + 128], newest, preferred_element_type=F)
             ).astype(BF)
             for k in range(2):
                 broad[pl.ds(rows, 8), pl.ds(REACH + cols + 16 * k, 16)] = middle[
                     :, SIDE * k : SIDE * (k + 1)
                 ].reshape(8, 16, SIDE)
-
-    def out_copy(step, half):
-        rows = 8 * (7 - step) if half == 0 else 8 * (8 + step)
-        return pltpu.make_async_copy(
-            out_slots.at[step, pl.ds(8 * half, 8)], sketch.at[pl.ds(rows, 8)], out_sem.at[step, half]
-        )
 
     def send_cols(step):
         for there, to_right in ((has_right, True), (has_left, False)):
@@ -306,26 +305,21 @@
                 def _():
                     col_copy(to_right, step, low).wait_recv()
 
-        @pl.loop(0, 8)
-        def _(index):
-            block = index // 4
-            rows = 8 * (7 - step + block * (1 + 2 * step)) + 2 * (index % 4)
-            pair = [broad[rows + k] for k in range(2)]
-            result = jnp.dot(
-                across[:, : SIDE + 2 * REACH],
-                jnp.concatenate(pair, axis=1),
-                preferred_element_type=F,
-            ).astype(BF)
-            slot = 2 * index
-            for k in range(2):
-                out_slots[step, slot + k] = result[:, SIDE * k : SIDE * (k + 1)]
-
-        flat = out_slots[step].reshape(16 * SIDE, SIDE)
-        gram_ref[...] += lax.dot_general(
-            flat, flat, (((0,), (0,)), ((), ())), preferred_element_type=F
-        )
-        for half in range(2):
-            out_copy(step, half).start()
+        for block in range(2):
+            rows = first_row(step, block)
+            for k in range(4):
+                pair = [broad[rows + 2 * k + m] for m in range(2)]
+                result = jnp.dot(
+                    across[:, : SIDE + 2 * REACH],
+                    jnp.concatenate(pair, axis=1),
+                    preferred_element_type=F,
+                ).astype(BF)
+                for m in range(2):
+                    sketch[rows + 2 * k + m] = result[:, SIDE * m : SIDE * (m + 1)]
+            flat = sketch[pl.ds(rows, 8)].reshape(8 * SIDE, SIDE)
+            gram_ref[...] += lax.dot_general(
+                flat, flat, (((0,), (0,)), ((), ())), preferred_element_type=F
+            )
 
     each_arrival(0, True)
     begin_rows(0)
@@ -408,8 +402,6 @@
 
     @pl.loop(0, STEPS)
     def _(step):
-        for half in range(2):
-            out_copy(step, half).wait()
         for there, to_right in ((has_right, True), (has_left, False)):
             for low in (True, False):
                 @pl.when(there)
@@ -426,16 +418,11 @@
             jax.ShapeDtypeStruct((SIDE, SIDE), BF),
             jax.ShapeDtypeStruct((1, 1, 4, SIDE, SIDE), F),
         ),
-        in_specs=[pl.BlockSpec(memory_space=pl.ANY)] * 3,
-        out_specs=(
-            pl.BlockSpec(memory_space=pl.ANY),
-            pl.BlockSpec(memory_space=pltpu.VMEM),
-            pl.BlockSpec(memory_space=pltpu.VMEM),
-        ),
+        in_specs=[pl.BlockSpec(memory_space=pltpu.HBM)] * 3,
+        out_specs=(pl.BlockSpec(memory_space=pltpu.VMEM),) * 3,
         scratch_shapes=[
             pltpu.VMEM((SIDE + 2 * REACH, SIDE, SIDE), BF),
             pltpu.VMEM((SIDE, SIDE + 2 * REACH, SIDE), BF),
-            pltpu.VMEM((STEPS, 16, SIDE, SIDE), BF),
             pltpu.VMEM((SIDE, 16 * depth), BF),
             pltpu.VMEM((SIDE, 384), BF),
             pltpu.VMEM((8, SIDE, 2 * SIDE), F),
@@ -448,7 +435,6 @@
             pltpu.VMEM((SIDE, SIDE), F),
             pltpu.SemaphoreType.DMA((2,)),
             pltpu.SemaphoreType.DMA,
-            pltpu.SemaphoreType.DMA((STEPS, 2)),
             pltpu.SemaphoreType.DMA((2, STEPS)),
             pltpu.SemaphoreType.DMA((2, STEPS)),
             pltpu.SemaphoreType.DMA((2, 2, STEPS)),
@@ -457,7 +443,7 @@
             pltpu.SemaphoreType.DMA((5,)),
         ],
         compiler_params=pltpu.CompilerParams(
-            collective_id=0, has_side_effects=True, vmem_limit_bytes=50 * 2**20
+            collective_id=0, has_side_effects=True, vmem_limit_bytes=48 * 2**20
         ),
         name="compress",
     )(taps, ranks, probes)
@@ -466,20 +452,13 @@
 CHUNKS = 8
 
 
-def basis_kernel(sketch, weights_ref, moved, out, moved_out, source, result, load_sem, store_sem, pass_sem):
+def basis_kernel(sketch, weights_ref, moved, out, moved_out, result, store_sem, pass_sem):
     rows = SIDE // CHUNKS
 
-    def part(ref, index):
-        return ref.at[pl.ds(rows * index, rows)]
-
-    def load(index):
-        return pltpu.make_async_copy(part(sketch, index), part(source, index), load_sem.at[index])
-
     def store(index):
-        return pltpu.make_async_copy(part(result, index), part(out, index), store_sem.at[index])
-
-    for index in range(CHUNKS):
-        load(index).start()
+        here = pl.ds(rows * index, rows)
+        return pltpu.make_async_copy(result.at[here], out.at[here], store_sem.at[index])
+
     forward = pltpu.make_async_copy(moved, moved_out, pass_sem)
     forward.start()
     weights = weights_ref[...]
@@ -490,11 +469,10 @@
 
     @pl.loop(0, CHUNKS)
     def _(index):
-        load(index).wait()
         half = rows // 2
         base = rows * index
         pair = [
-            source[pl.ds(base + half * k, half)].reshape(half * SIDE, SIDE) for k in range(2)
+            sketch[pl.ds(base + half * k, half)].reshape(half * SIDE, SIDE) for k in range(2)
         ]
         both = jnp.dot(jnp.concatenate(pair, axis=1), twice, preferred_element_type=F).astype(BF)
         for k in range(2):
@@ -509,23 +487,20 @@
 
 
 def basis(sketch, weights, moved):
-    anywhere = pl.BlockSpec(memory_space=pl.ANY)
     return pl.pallas_call(
         basis_kernel,
         out_shape=(
             jax.ShapeDtypeStruct(sketch.shape, BF),
             jax.ShapeDtypeStruct(moved.shape, F),
         ),
-        in_specs=[anywhere, pl.BlockSpec(memory_space=pltpu.VMEM), anywhere],
-        out_specs=(anywhere, anywhere),
+        in_specs=[pl.BlockSpec(memory_space=pltpu.VMEM)] * 3,
+        out_specs=(pl.BlockSpec(memory_space=pltpu.HBM),) * 2,
         scratch_shapes=[
             pltpu.VMEM(sketch.shape, BF),
-            pltpu.VMEM(sketch.shape, BF),
-            pltpu.SemaphoreType.DMA((CHUNKS,)),
             pltpu.SemaphoreType.DMA((CHUNKS,)),
             pltpu.SemaphoreType.DMA,
         ],
-        compiler_params=pltpu.CompilerParams(vmem_limit_bytes=24 * 2**20),
+        compiler_params=pltpu.CompilerParams(vmem_limit_bytes=16 * 2**20),
         name="basis",
     )(sketch, weights, moved)
 

time: 118 us -> 107 us (0.907)
  Pallas kernels: 114 us -> 105 us
  local copies, waits for them, and re-layouts: 3.58 us -> 1.4 us
    pallas_call x1, Pallas kernels: 110 us -> 101 us  [compress(): pl.pallas_call(body, out_shape=(jax.ShapeDtypeStruct((SIDE, SIDE, SIDE),...]
    unnamed x6 -> x4, local copies, waits for them, and re-layouts: 3.58 us -> 1.4 us
where the time goes in v4:
time: 107 us
  Pallas kernels  105 us (98%)
  local copies, waits for them, and re-layouts  1.4 us (1%)
    pallas_call x1, Pallas kernels, compress(): pl.pallas_call(body, out_shape=(jax.ShapeDtypeStruct((SIDE, SIDE, SIDE),...  101 us
    pallas_call x1, Pallas kernels, basis(): pl.pallas_call(basis_kernel, out_shape=(jax.ShapeDtypeStruct(sketch.shape...  3.29 us

profile of v4, /device:TPU:96, one launch (start us, length us, event | category | flops | bytes accessed | tf_op | source)
XLA Modules:
  0.0 106.8 jit_solution(14826540688104593244)
XLA Ops:
  0.6 0.0 copy-start
  0.6 0.7 copy-done
  1.4 0.0 copy-start.1
  1.4 0.7 copy-done.1
  2.0 101.4 %compress.1 = (bf16[128,128,128]{2,1,0:T(8,128)(2,1)S(1)}, bf16[128,128]{1,0:T(8,128)(2,1)S(1)}, f32[1,1,4,128,128]{4,3,2,1,0:T(8,128)S(1)}) custom-call(f32[2,2,33]{2,1,0:T(2,128)S(1)} %copy-done.1, s32[5,8,32]{2,1,0:T(8,128)S(1)} %bitcast.1, bf16[128,128,128]{2,1,0:T(8,128)(2,1)} %probes.1), custom_call_target="tpu_custom_call" | custom-call | tf_op jit(solution)/shard_map/compress/pallas_call | solution.py:414
  103.5 3.3 %basis.1 = (bf16[128,128,128]{2,1,0:T(8,128)(2,1)}, f32[1,1,4,128,128]{4,3,2,1,0:T(8,128)}) custom-call(bf16[128,128,128]{2,1,0:T(8,128)(2,1)S(1)} %get-tuple-element.5.sketch, bf16[128,128]{1,0:T(8,128)(2,1)S(1)} %get-tuple-element.6.weights_ref, f32[1,1,4,128,128]{4,3,2,1,0:T(8,128)S(1)} %get-tuple-element.7.moved), custom_call_target="tpu_custom_call" | custom-call | tf_op jit(solution)/shard_map/basis/pallas_call | solution.py:490
Async XLA Ops:
  0.6 0.7 copy-start
  1.4 0.7 copy-start.1

commit v5 on v4

--- a/solution.py
+++ b/solution.py
@@ -29,46 +29,56 @@
     return one, two, (rest - two.astype(F)).astype(BF)
 
 
-def eliminate(tiles):
+def eliminate(tiles, extra, emit):
     sub = lax.broadcasted_iota(jnp.int32, (8, 128), 0)
     lane = lax.broadcasted_iota(jnp.int32, (8, 128), 1)
-    tiles, out = list(tiles), []
+    zero = jnp.zeros((8, 128), F)
+    sets = [list(tiles)] + ([list(extra)] if extra is not None else [])
+    tiles = sets[0]
     for b in range(8):
         j = 16 * b
-        rows = [tiles[2 * b], tiles[2 * b + 1]]
-        cols = [[lane_of(rows[h], j + c) for c in range(16)] for h in range(2)]
         near = range(2 * b + 2, min(2 * b + 4, 16))
-        below = {t: [lane_of(tiles[t], j + c) for c in range(16)] for t in near}
-        a1, a2, a3 = split(jnp.concatenate(rows, axis=0))
+        body = [2 * b, 2 * b + 1, *near]
+        cols = {
+            t: [lane_of(tiles[t], j + c) if t > 2 * b or c < 8 else None for c in range(16)]
+            for t in body
+        }
         inside = (lane >= j) & (lane < j + 16)
-        rows = [
-            jnp.where(inside, jnp.where(lane - j == sub + 8 * h, 1.0, 0.0), rows[h]) for h in range(2)
-        ]
-        kept = [jnp.zeros((8, 128), F) for _ in range(2)]
+        for t in body:
+            h = t - 2 * b
+            unit = jnp.where(lane - j == sub + 8 * h, 1.0, 0.0) if h < 2 else 0.0
+            tiles[t] = jnp.where(inside, unit, tiles[t])
+        kept = [[zero, zero] for _ in sets]
+        raw, scaled = [zero, zero], [[zero, zero] for _ in sets]
         for c in range(16):
             h, s = divmod(c, 8)
-            pivot = row_of(cols[h][c], s)
-            inv = 1.0 / pivot
-            line = row_of(rows[h], s)
-            kept[h] = jnp.where(sub == s, line * lax.rsqrt(pivot), kept[h])
-            line = line * inv
-            for g in range(2):
-                new = rows[g] - cols[g][c] * line
-                rows[g] = jnp.where(sub == s, line, new) if g == h else new
-            for e in range(c + 1, 16):
-                line_e = row_of(cols[h][e], s) * inv
-                for g in range(2):
-                    new = cols[g][e] - cols[g][c] * line_e
-                    cols[g][e] = jnp.where(sub == s, line_e, new) if g == h else new
-        out += [jnp.where(lane <= j + 8 * h + sub, kept[h], 0.0) for h in range(2)]
-        lines = [row_of(rows[c // 8], c % 8) for c in range(16)]
-        for t in near:
-            terms = [below[t][c] * lines[c] for c in range(16)]
-            while len(terms) > 1:
-                terms = [terms[i] + terms[i + 1] for i in range(0, len(terms), 2)]
-            tiles[t] = jnp.where(inside, 0.0, tiles[t]) - terms[0]
+            first = 2 * b + h
+            pivot = row_of(cols[first][c], s)
+            inv, root = 1.0 / pivot, lax.rsqrt(pivot)
+            lines = [row_of(one[first], s) for one in sets]
+            for k, line in enumerate(lines):
+                kept[k][h] = jnp.where(sub == s, line * root, kept[k][h])
+                if b < 6:
+                    scaled[k][h] = jnp.where(sub == s, line * inv, scaled[k][h])
+            if b < 6:
+                raw[h] = jnp.where(sub == s, lines[0], raw[h])
+            for t in body[h:]:
+                ratio = cols[t][c] * inv
+                for e in range(c + 1, 16):
+                    if t >= 2 * b + e // 8:
+                        entry = row_of(cols[2 * b + e // 8][c], e % 8)
+                        cols[t][e] = cols[t][e] - ratio * entry
+                for k, line in enumerate(lines):
+                    sets[k][t] = sets[k][t] - ratio * line
+        emit(
+            b,
+            [jnp.where(lane <= j + 8 * h + sub, kept[0][h], 0.0) for h in range(2)],
+            kept[1] if len(sets) > 1 else None,
+        )
         if b < 6:
-            b1, b2, b3 = split(jnp.concatenate(rows, axis=0))
+            a1, a2, a3 = split(jnp.concatenate(raw, axis=0))
+            wide = [jnp.concatenate(pair, axis=0) for pair in scaled]
+            b1, b2, b3 = split(jnp.concatenate(wide, axis=1))
             change = lax.dot_general(
                 jnp.concatenate([a1, a1, a2, a2, a1, a3], axis=0),
                 jnp.concatenate([b1, b2, b1, b2, b3, b1], axis=0),
@@ -76,24 +86,33 @@
                 preferred_element_type=F,
             )
             for t in range(2 * b + 4, 16):
-                tiles[t] = jnp.where(inside, 0.0, tiles[t]) - change[8 * t : 8 * t + 8]
-    return out
-
-
-def factor(g, rank):
-    row=lax.broadcasted_iota(jnp.int32,(128,128),0); col=lax.broadcasted_iota(jnp.int32,(128,128),1)
-    keep=(row.astype(F)<rank)&(col.astype(F)<rank)
-    masked=jnp.where(keep,g,0.0)
-    eye=row==col
-    trace=jnp.sum(jnp.where(eye,masked,0.0),keepdims=True)
-    delta=0.01*trace/rank
-    a=masked*(1.0/delta)+jnp.where(eye,1.0,0.0)
-    linv=jnp.concatenate(eliminate([a[8*t:8*t+8] for t in range(16)]),axis=0)
-    linv=jnp.where(keep,linv*lax.rsqrt(delta),0.0)
-    return masked, linv
-
-def dot(a, b):
-    return jnp.dot(a, b, precision=HIGHEST, preferred_element_type=F)
+                tiles[t] = jnp.where(inside, 0.0, tiles[t])
+                for k, one in enumerate(sets):
+                    one[t] = one[t] - change[8 * t : 8 * t + 8, 128 * k : 128 * k + 128]
+
+
+def factor(gram, rank, emit=None):
+    row = lax.broadcasted_iota(jnp.int32, (128, 128), 0)
+    col = lax.broadcasted_iota(jnp.int32, (128, 128), 1)
+    keep = (row < rank) & (col < rank)
+    masked = jnp.where(keep, gram, 0.0)
+    eye = row == col
+    trace = jnp.sum(jnp.where(eye, masked, 0.0), keepdims=True)
+    delta = 0.01 * trace / jnp.full((1, 1), rank, jnp.int32).astype(F)
+    shifted = masked * (1.0 / delta) + jnp.where(eye, 1.0, 0.0)
+    root = jnp.broadcast_to(lax.rsqrt(delta), (16, 128))
+    out = []
+
+    def take(b, inverse, solved):
+        out.append(jnp.concatenate(inverse, axis=0) * root)
+        if emit is not None:
+            emit(b, jnp.concatenate(solved, axis=0) * root)
+
+    def tiles(a):
+        return [a[8 * t : 8 * t + 8] for t in range(16)]
+
+    eliminate(tiles(shifted), tiles(masked) if emit is not None else None, take)
+    return jnp.where(keep, jnp.concatenate(out, axis=0), 0.0)
 
 
 def dot_tn(a, b):
@@ -112,17 +131,22 @@
     return row, col
 
 
-def combine(taps, pads):
-    pads[...] = jnp.zeros_like(pads)
-    for which in range(2):
-        for dim in range(2):
-            pads[which, dim : dim + 1, 0 : taps.shape[2]] = taps[dim, which : which + 1, :]
-    first, second = pads[0], pads[1]
-    total = jnp.zeros_like(first)
-    for b in range(taps.shape[2]):
-        moved = pltpu.roll(first, 4 * b, 1) if b else first
-        total = total + moved * jnp.broadcast_to(second[:, b : b + 1], first.shape)
+def combine(taps):
+    sub = lax.broadcasted_iota(jnp.int32, (16, 256), 0)
+    lane = lax.broadcasted_iota(jnp.int32, (16, 256), 1)
+    count = taps.shape[2]
+
+    def of(which, index):
+        return jnp.where(sub == 0, taps[0, which, index], taps[1, which, index])
+
+    first = jnp.zeros((16, 256), F)
+    for a in range(count):
+        first = jnp.where(lane == a, of(0, a), first)
+    total = jnp.zeros((16, 256), F)
+    for b in range(count):
+        total = total + (pltpu.roll(first, 4 * b, 1) if b else first) * of(1, b)
     return total.astype(BF)
+
 
 def stretched(line, length, width):
     sub = lax.broadcasted_iota(jnp.int32, (8, width), 0)
@@ -135,8 +159,8 @@
 
 def body(
     taps, ranks, probes, sketch, weights_ref, moved_ref,
-    tall, broad, mix, across, part, gram_ref, taps_ref, ranks_ref, pads, own, other, zeta_ref,
-    small_sem, own_sem, row_send, row_recv, col_send, col_recv, swap_send, swap_recv,
+    tall, broad, mix, across, part, gram_ref, own, other,
+    own_sem, row_send, row_recv, col_send, col_recv, swap_send, swap_recv,
 ):
     n_x, n_y = lax.axis_size("tx"), lax.axis_size("ty")
     row_at, col_at = lax.axis_index("tx"), lax.axis_index("ty")
@@ -148,12 +172,6 @@
 
     load = pltpu.make_async_copy(probes, tall.at[pl.ds(REACH, SIDE)], own_sem)
     load.start()
-    small = [
-        pltpu.make_async_copy(taps, taps_ref, small_sem.at[0]),
-        pltpu.make_async_copy(ranks, ranks_ref, small_sem.at[1]),
-    ]
-    for copy in small:
-        copy.start()
     barrier = pltpu.get_barrier_semaphore()
     for there, device in sides:
         @pl.when(there)
@@ -217,9 +235,7 @@
     sent = lambda copy: copy.wait_send()
     each(start, 0, True)
     each(start, 1)
-    for copy in small:
-        copy.wait()
-    lines = combine(taps_ref, pads)
+    lines = combine(taps)
     wide = mix.shape[1]
     spot = lax.broadcasted_iota(jnp.int32, (256, wide), 1)
     spread = jnp.where(spot == 16 * lax.broadcasted_iota(jnp.int32, (256, wide), 0), 1.0, 0.0)
@@ -354,51 +370,52 @@
 
     filter_cols(STEPS - 1)
 
-    def swap(level):
+    def swap(level, b):
+        here = pl.ds(16 * b, 16)
         return pltpu.make_async_remote_copy(
-            src_ref=own.at[level],
-            dst_ref=other.at[level],
-            send_sem=swap_send.at[level],
-            recv_sem=swap_recv.at[level],
-            device_id=partner_of(level, row_at, col_at),
+            src_ref=own.at[level, here],
+            dst_ref=other.at[level, here],
+            send_sem=swap_send.at[level, b],
+            recv_sem=swap_recv.at[level, b],
+            device_id=partner_of(level + 1, row_at, col_at),
             device_id_type=MESH,
         )
 
-    def rank_at(level, row, col):
-        table = ranks_ref[level]
-        spot = (lax.broadcasted_iota(jnp.int32, table.shape, 0) == col) & (
-            lax.broadcasted_iota(jnp.int32, table.shape, 1) == row
-        )
-        return jnp.sum(jnp.where(spot, table, 0).astype(F), keepdims=True)
-
-    masked, linv = factor(gram_ref[...] * (1.0 / (SIDE * SIDE)), rank_at(0, row_at, col_at))
-    zeta = dot(linv, masked)
-    zeta_ref[...] = zeta
-    own[1] = dot_tn(zeta, zeta)
-    swap(1).start()
-    weights_ref[...] = linv.T.astype(BF)
-
-    @pl.loop(1, 5)
+    def rank_at(level, span_x, span_y):
+        return ranks[level, col_at - col_at % span_y, row_at - row_at % span_x]
+
+    gram_ref[...] = gram_ref[...] * (1.0 / (SIDE * SIDE))
+
+    @pl.loop(0, 4)
     def _(level):
-        span_x = jnp.where(level < 3, 2, 4)
-        span_y = jnp.where(level < 2, 1, jnp.where(level < 4, 2, 4))
-        rank = rank_at(level, row_at - row_at % span_x, col_at - col_at % span_y)
-        swap(level).wait_recv()
-        masked, linv = factor((own[level] + other[level]) * 0.5, rank)
-        child = zeta_ref[...]
-
-        @pl.when(level < 4)
-        def _():
-            zeta = dot(linv, masked)
-            zeta_ref[...] = zeta
-            own[level + 1] = dot_tn(zeta, zeta)
-            swap(level + 1).start()
-
-        moved_ref[0, 0, level - 1] = dot_nt(child, linv)
-
-    @pl.loop(1, 5)
+        span_x = jnp.where(level < 1, 1, jnp.where(level < 3, 2, 4))
+        span_y = jnp.where(level < 2, 1, 2)
+
+        def emit(b, solved):
+            own[level, 16 * b : 16 * b + 16] = solved
+            swap(level, b).start()
+
+        linv = factor(gram_ref[...], rank_at(level, span_x, span_y), emit)
+
+        @pl.when(level == 0)
+        def _():
+            weights_ref[...] = linv.T.astype(BF)
+
+        @pl.when(level > 0)
+        def _():
+            moved_ref[0, 0, level - 1] = dot_nt(own[level - 1], linv)
+        for b in range(8):
+            swap(level, b).wait_recv()
+        both = jnp.concatenate([own[level], other[level]], axis=0)
+        gram_ref[...] = dot_tn(both, both) * 0.5
+
+    linv = factor(gram_ref[...], rank_at(4, 4, 4))
+    moved_ref[0, 0, 3] = dot_nt(own[3], linv)
+
+    @pl.loop(0, 4)
     def _(level):
-        swap(level).wait_send()
+        for b in range(8):
+            swap(level, b).wait_send()
 
     @pl.loop(0, STEPS)
     def _(step):
@@ -418,7 +435,11 @@
             jax.ShapeDtypeStruct((SIDE, SIDE), BF),
             jax.ShapeDtypeStruct((1, 1, 4, SIDE, SIDE), F),
         ),
-        in_specs=[pl.BlockSpec(memory_space=pltpu.HBM)] * 3,
+        in_specs=[
+            pl.BlockSpec(memory_space=pltpu.SMEM),
+            pl.BlockSpec(memory_space=pltpu.SMEM),
+            pl.BlockSpec(memory_space=pltpu.HBM),
+        ],
         out_specs=(pl.BlockSpec(memory_space=pltpu.VMEM),) * 3,
         scratch_shapes=[
             pltpu.VMEM((SIDE + 2 * REACH, SIDE, SIDE), BF),
@@ -427,20 +448,15 @@
             pltpu.VMEM((SIDE, 384), BF),
             pltpu.VMEM((8, SIDE, 2 * SIDE), F),
             pltpu.VMEM((SIDE, SIDE), F),
-            pltpu.VMEM(taps.shape, F),
-            pltpu.VMEM(ranks.shape, jnp.int32),
-            pltpu.VMEM((2, 16, 256), F),
-            pltpu.VMEM((5, SIDE, SIDE), F),
-            pltpu.VMEM((5, SIDE, SIDE), F),
-            pltpu.VMEM((SIDE, SIDE), F),
-            pltpu.SemaphoreType.DMA((2,)),
+            pltpu.VMEM((4, SIDE, SIDE), F),
+            pltpu.VMEM((4, SIDE, SIDE), F),
             pltpu.SemaphoreType.DMA,
             pltpu.SemaphoreType.DMA((2, STEPS)),
             pltpu.SemaphoreType.DMA((2, STEPS)),
             pltpu.SemaphoreType.DMA((2, 2, STEPS)),
             pltpu.SemaphoreType.DMA((2, 2, STEPS)),
-            pltpu.SemaphoreType.DMA((5,)),
-            pltpu.SemaphoreType.DMA((5,)),
+            pltpu.SemaphoreType.DMA((4, 8)),
+            pltpu.SemaphoreType.DMA((4, 8)),
         ],
         compiler_params=pltpu.CompilerParams(
             collective_id=0, has_side_effects=True, vmem_limit_bytes=48 * 2**20

time: 107 us -> 105 us (0.981)
  Pallas kernels: 105 us -> 102 us
    pallas_call x1, Pallas kernels: 101 us -> 99.2 us  [compress(): pl.pallas_call(body, out_shape=(jax.ShapeDtypeStruct((SIDE, SIDE, SIDE),...]
where the time goes in v5:
time: 105 us
  Pallas kernels  102 us (97%)
  local copies, waits for them, and re-layouts  1.4 us (1%)
    pallas_call x1, Pallas kernels, compress(): pl.pallas_call(body, out_shape=(jax.ShapeDtypeStruct((SIDE, SIDE, SIDE),...  99.2 us
    pallas_call x1, Pallas kernels, basis(): pl.pallas_call(basis_kernel, out_shape=(jax.ShapeDtypeStruct(sketch.shape...  3.28 us

profile of v5, /device:TPU:96, one launch (start us, length us, event | category | flops | bytes accessed | tf_op | source)
XLA Modules:
  0.0 104.5 jit_solution(3059921533976319658)
XLA Ops:
  0.6 0.0 copy-start
  0.6 0.7 copy-done
  1.4 0.0 copy-start.1
  1.4 0.7 copy-done.1
  2.0 99.2 %compress.1 = (bf16[128,128,128]{2,1,0:T(8,128)(2,1)S(1)}, bf16[128,128]{1,0:T(8,128)(2,1)S(1)}, f32[1,1,4,128,128]{4,3,2,1,0:T(8,128)S(1)}) custom-call(f32[2,2,33]{2,1,0:T(2,128)S(1)} %copy-done.1, s32[5,8,32]{2,1,0:T(8,128)S(1)} %bitcast.1, bf16[128,128,128]{2,1,0:T(8,128)(2,1)} %probes.1), custom_call_target="tpu_custom_call" | custom-call | tf_op jit(solution)/shard_map/compress/pallas_call | solution.py:431
  101.3 3.3 %basis.1 = (bf16[128,128,128]{2,1,0:T(8,128)(2,1)}, f32[1,1,4,128,128]{4,3,2,1,0:T(8,128)}) custom-call(bf16[128,128,128]{2,1,0:T(8,128)(2,1)S(1)} %get-tuple-element.5.sketch, bf16[128,128]{1,0:T(8,128)(2,1)S(1)} %get-tuple-element.6.weights_ref, f32[1,1,4,128,128]{4,3,2,1,0:T(8,128)S(1)} %get-tuple-element.7.moved), custom_call_target="tpu_custom_call" | custom-call | tf_op jit(solution)/shard_map/basis/pallas_call | solution.py:506
Async XLA Ops:
  0.6 0.7 copy-start
  1.4 0.7 copy-start.1

commit v6 on v5

--- a/solution.py
+++ b/solution.py
@@ -158,9 +158,9 @@
 
 
 def body(
-    taps, ranks, probes, sketch, weights_ref, moved_ref,
-    tall, broad, mix, across, part, gram_ref, own, other,
-    own_sem, row_send, row_recv, col_send, col_recv, swap_send, swap_recv,
+    taps_far, ranks_far, probes, sketch, weights_ref, moved_ref,
+    tall, broad, mix, across, part, gram_ref, own, other, taps, ranks,
+    small_sem, own_sem, row_send, row_recv, col_send, col_recv, swap_send, swap_recv,
 ):
     n_x, n_y = lax.axis_size("tx"), lax.axis_size("ty")
     row_at, col_at = lax.axis_index("tx"), lax.axis_index("ty")
@@ -172,6 +172,12 @@
 
     load = pltpu.make_async_copy(probes, tall.at[pl.ds(REACH, SIDE)], own_sem)
     load.start()
+    small = [
+        pltpu.make_async_copy(taps_far, taps, small_sem.at[0]),
+        pltpu.make_async_copy(ranks_far, ranks, small_sem.at[1]),
+    ]
+    for copy in small:
+        copy.start()
     barrier = pltpu.get_barrier_semaphore()
     for there, device in sides:
         @pl.when(there)
@@ -187,9 +193,20 @@
     peers = [there.astype(jnp.int32) for there, _ in sides]
     pl.semaphore_wait(barrier, peers[0] + peers[1] + peers[2] + peers[3] + 4)
 
+    def is_last(step):
+        return isinstance(step, int) and step >= STEPS - 1
+
+    def size_of(step):
+        return 4 if is_last(step) else 8
+
+    def first_row(step, block):
+        if is_last(step):
+            return (4, 120)[block] if step == STEPS - 1 else (0, 124)[block]
+        return pl.multiple_of(8 * (7 - step + block * (1 + 2 * step)), 8)
+
     def row_copy(to_down, step, first):
-        count = 24 if first else 8
-        far = 8 * step + 24
+        count = 24 if first else size_of(step)
+        far = 48 + 4 * step if is_last(step) else 8 * step + 24
         if to_down:
             source, target, device, way = SIDE - far, REACH - far, down, 0
         else:
@@ -204,15 +221,15 @@
         )
 
     def col_copy(to_right, step, low):
-        rows = 8 * (7 - step) if low else 8 * (8 + step)
+        rows, count = first_row(step, 0 if low else 1), size_of(step)
         if to_right:
             source, target, device, way = SIDE, 0, right, 0
         else:
             source, target, device, way = REACH, REACH + SIDE, left, 1
         half = 0 if low else 1
         return pltpu.make_async_remote_copy(
-            src_ref=broad.at[pl.ds(rows, 8), pl.ds(source, REACH)],
-            dst_ref=broad.at[pl.ds(rows, 8), pl.ds(target, REACH)],
+            src_ref=broad.at[pl.ds(rows, count), pl.ds(source, REACH)],
+            dst_ref=broad.at[pl.ds(rows, count), pl.ds(target, REACH)],
             send_sem=col_send.at[way, half, step],
             recv_sem=col_recv.at[way, half, step],
             device_id=device,
@@ -235,6 +252,8 @@
     sent = lambda copy: copy.wait_send()
     each(start, 0, True)
     each(start, 1)
+    for copy in small:
+        copy.wait()
     lines = combine(taps)
     wide = mix.shape[1]
     spot = lax.broadcasted_iota(jnp.int32, (256, wide), 1)
@@ -263,11 +282,9 @@
     gram_ref[...] = jnp.zeros_like(gram_ref)
     load.wait()
 
-    def first_row(step, block):
-        return pl.multiple_of(8 * (7 - step + block * (1 + 2 * step)), 8)
-
     def place(step, block, group):
-        return 4 * block + group, first_row(step, block), 32 * group
+        rows = pl.multiple_of(8 * (7 - step + block * (1 + 2 * step)), 8)
+        return 4 * block + group, rows, 32 * group
 
     def aligned(cols):
         return cols if isinstance(cols, int) else pl.multiple_of(cols, 16)
@@ -307,6 +324,29 @@
                     :, SIDE * k : SIDE * (k + 1)
                 ].reshape(8, 16, SIDE)
 
+    def finish_last(step):
+        second = step == STEPS
+        for block, group in [(block, group) for block in range(2) for group in range(4)]:
+            depth = 8 if second else 4
+            half = 64 * (second == (block == 1))
+            start_row = 0 if block == 0 else REACH + SIDE + REACH - 8
+            shift = 0 if second or block == 1 else 4
+            offset = 16 * (2 * REACH * block + shift)
+            newest = columns(start_row + shift, depth, 32 * group)
+            middle = (
+                part[4 * block + group, half : half + 64]
+                + jnp.dot(
+                    mix[half : half + 64, offset : offset + 16 * depth],
+                    newest,
+                    preferred_element_type=F,
+                )
+            ).astype(BF)
+            rows = first_row(step, block)
+            for k in range(2):
+                broad[pl.ds(rows, 4), pl.ds(REACH + 32 * group + 16 * k, 16)] = middle[
+                    :, SIDE * k : SIDE * (k + 1)
+                ].reshape(4, 16, SIDE)
+
     def send_cols(step):
         for there, to_right in ((has_right, True), (has_left, False)):
             for low in (True, False):
@@ -323,7 +363,7 @@
 
         for block in range(2):
             rows = first_row(step, block)
-            for k in range(4):
+            for k in range(size_of(step) // 2):
                 pair = [broad[rows + 2 * k + m] for m in range(2)]
                 result = jnp.dot(
                     across[:, : SIDE + 2 * REACH],
@@ -332,7 +372,7 @@
                 ).astype(BF)
                 for m in range(2):
                     sketch[rows + 2 * k + m] = result[:, SIDE * m : SIDE * (m + 1)]
-            flat = sketch[pl.ds(rows, 8)].reshape(8 * SIDE, SIDE)
+            flat = sketch[pl.ds(rows, size_of(step))].reshape(size_of(step) * SIDE, SIDE)
             gram_ref[...] += lax.dot_general(
                 flat, flat, (((0,), (0,)), ((), ())), preferred_element_type=F
             )
@@ -340,7 +380,7 @@
     each_arrival(0, True)
     begin_rows(0)
 
-    @pl.loop(0, STEPS)
+    @pl.loop(0, STEPS - 1)
     def _(step):
         @pl.when(step > 0)
         def _():
@@ -356,19 +396,34 @@
         def _():
             each(sent, step)
 
-        @pl.when(step < STEPS - 2)
+        @pl.when(step < STEPS - 3)
         def _():
             each(start, step + 2)
 
-        @pl.when(step < STEPS - 1)
-        def _():
-            begin_rows(step + 1)
+        @pl.when(step == STEPS - 3)
+        def _():
+            each(start, STEPS - 1)
+
+        @pl.when(step == STEPS - 2)
+        def _():
+            each(start, STEPS)
+
+        begin_rows(step + 1)
 
         @pl.when(step > 0)
         def _():
             filter_cols(step - 1)
 
-    filter_cols(STEPS - 1)
+    last = (STEPS - 1, STEPS)
+    for step in last:
+        each_arrival(step)
+        finish_last(step)
+        send_cols(step)
+        if step == last[0]:
+            filter_cols(jnp.int32(STEPS - 2))
+    for step in last:
+        filter_cols(step)
+        each(sent, step)
 
     def swap(level, b):
         here = pl.ds(16 * b, 16)
@@ -417,13 +472,19 @@
         for b in range(8):
             swap(level, b).wait_send()
 
-    @pl.loop(0, STEPS)
-    def _(step):
+    def sent_cols(step):
         for there, to_right in ((has_right, True), (has_left, False)):
             for low in (True, False):
                 @pl.when(there)
                 def _():
                     col_copy(to_right, step, low).wait_send()
+
+    @pl.loop(0, STEPS - 1)
+    def _(step):
+        sent_cols(step)
+
+    for step in last:
+        sent_cols(step)
 
 
 def compress(taps, ranks, probes):
@@ -436,8 +497,8 @@
             jax.ShapeDtypeStruct((1, 1, 4, SIDE, SIDE), F),
         ),
         in_specs=[
-            pl.BlockSpec(memory_space=pltpu.SMEM),
-            pl.BlockSpec(memory_space=pltpu.SMEM),
+            pl.BlockSpec(memory_space=pltpu.HBM),
+            pl.BlockSpec(memory_space=pltpu.HBM),
             pl.BlockSpec(memory_space=pltpu.HBM),
         ],
         out_specs=(pl.BlockSpec(memory_space=pltpu.VMEM),) * 3,
@@ -450,11 +511,14 @@
             pltpu.VMEM((SIDE, SIDE), F),
             pltpu.VMEM((4, SIDE, SIDE), F),
             pltpu.VMEM((4, SIDE, SIDE), F),
+            pltpu.SMEM(taps.shape, F),
+            pltpu.SMEM(ranks.shape, jnp.int32),
+            pltpu.SemaphoreType.DMA((2,)),
             pltpu.SemaphoreType.DMA,
-            pltpu.SemaphoreType.DMA((2, STEPS)),
-            pltpu.SemaphoreType.DMA((2, STEPS)),
-            pltpu.SemaphoreType.DMA((2, 2, STEPS)),
-            pltpu.SemaphoreType.DMA((2, 2, STEPS)),
+            pltpu.SemaphoreType.DMA((2, STEPS + 1)),
+            pltpu.SemaphoreType.DMA((2, STEPS + 1)),
+            pltpu.SemaphoreType.DMA((2, 2, STEPS + 1)),
+            pltpu.SemaphoreType.DMA((2, 2, STEPS + 1)),
             pltpu.SemaphoreType.DMA((4, 8)),
             pltpu.SemaphoreType.DMA((4, 8)),
         ],
@@ -462,7 +526,7 @@
             collective_id=0, has_side_effects=True, vmem_limit_bytes=48 * 2**20
         ),
         name="compress",
-    )(taps, ranks, probes)
+    )(*[pltpu.with_memory_space_constraint(a, pltpu.HBM) for a in (taps, ranks)], probes)
 
 
 CHUNKS = 8

time: 105 us -> 103 us (0.981)
  local copies, waits for them, and re-layouts: 1.4 us -> 0 us
    unnamed x4 -> x0, local copies, waits for them, and re-layouts: 1.4 us -> none
where the time goes in v6:
time: 103 us
  Pallas kernels  102 us (99%)
    pallas_call x1, Pallas kernels, compress(): pl.pallas_call(body, out_shape=(jax.ShapeDtypeStruct((SIDE, SIDE, SIDE),...  98.7 us
    pallas_call x1, Pallas kernels, basis(): pl.pallas_call(basis_kernel, out_shape=(jax.ShapeDtypeStruct(sketch.shape...  3.29 us

profile of v6, /device:TPU:96, one launch (start us, length us, event | category | flops | bytes accessed | tf_op | source)
XLA Modules:
  0.0 102.6 jit_solution(8547769730372522745)
XLA Ops:
  0.6 98.7 %compress.1 = (bf16[128,128,128]{2,1,0:T(8,128)(2,1)S(1)}, bf16[128,128]{1,0:T(8,128)(2,1)S(1)}, f32[1,1,4,128,128]{4,3,2,1,0:T(8,128)S(1)}) custom-call(f32[2,2,33]{2,1,0:T(2,128)} %taps_far.1, s32[5,8,32]{2,1,0:T(8,128)} %bitcast.1, bf16[128,128,128]{2,1,0:T(8,128)(2,1)} %probes.1), custom_call_target="tpu_custom_call" | custom-call | tf_op jit(solution)/shard_map/compress/pallas_call | solution.py:492
  99.3 3.3 %basis.1 = (bf16[128,128,128]{2,1,0:T(8,128)(2,1)}, f32[1,1,4,128,128]{4,3,2,1,0:T(8,128)}) custom-call(bf16[128,128,128]{2,1,0:T(8,128)(2,1)S(1)} %get-tuple-element.5.sketch, bf16[128,128]{1,0:T(8,128)(2,1)S(1)} %get-tuple-element.6.weights_ref, f32[1,1,4,128,128]{4,3,2,1,0:T(8,128)S(1)} %get-tuple-element.7.moved), custom_call_target="tpu_custom_call" | custom-call | tf_op jit(solution)/shard_map/basis/pallas_call | solution.py:570

commit v7 on v6

--- a/solution.py
+++ b/solution.py
@@ -158,8 +158,8 @@
 
 
 def body(
-    taps_far, ranks_far, probes, sketch, weights_ref, moved_ref,
-    tall, broad, mix, across, part, gram_ref, own, other, taps, ranks,
+    taps_far, ranks_far, probes, sketch, moved_ref,
+    tall, broad, mix, across, part, gram_ref, weights_ref, own, other, taps, ranks,
     small_sem, own_sem, row_send, row_recv, col_send, col_recv, swap_send, swap_recv,
 ):
     n_x, n_y = lax.axis_size("tx"), lax.axis_size("ty")
@@ -459,6 +459,23 @@
         @pl.when(level > 0)
         def _():
             moved_ref[0, 0, level - 1] = dot_nt(own[level - 1], linv)
+        weights = weights_ref[...]
+        zero = jnp.zeros_like(weights)
+        twice = jnp.concatenate(
+            [
+                jnp.concatenate([weights, zero], axis=1),
+                jnp.concatenate([zero, weights], axis=1),
+            ],
+            axis=0,
+        )
+        for group in range(4):
+            rows = pl.multiple_of(32 * level + 8 * group, 8)
+            pair = [sketch[pl.ds(rows + 4 * k, 4)].reshape(4 * SIDE, SIDE) for k in range(2)]
+            both = jnp.dot(jnp.concatenate(pair, axis=1), twice, preferred_element_type=F)
+            for k in range(2):
+                sketch[pl.ds(rows + 4 * k, 4)] = (
+                    both[:, SIDE * k : SIDE * (k + 1)].astype(BF).reshape(4, SIDE, SIDE)
+                )
         for b in range(8):
             swap(level, b).wait_recv()
         both = jnp.concatenate([own[level], other[level]], axis=0)
@@ -493,7 +510,6 @@
         body,
         out_shape=(
             jax.ShapeDtypeStruct((SIDE, SIDE, SIDE), BF),
-            jax.ShapeDtypeStruct((SIDE, SIDE), BF),
             jax.ShapeDtypeStruct((1, 1, 4, SIDE, SIDE), F),
         ),
         in_specs=[
@@ -501,7 +517,7 @@
             pl.BlockSpec(memory_space=pltpu.HBM),
             pl.BlockSpec(memory_space=pltpu.HBM),
         ],
-        out_specs=(pl.BlockSpec(memory_space=pltpu.VMEM),) * 3,
+        out_specs=(pl.BlockSpec(memory_space=pltpu.VMEM),) * 2,
         scratch_shapes=[
             pltpu.VMEM((SIDE + 2 * REACH, SIDE, SIDE), BF),
             pltpu.VMEM((SIDE, SIDE + 2 * REACH, SIDE), BF),
@@ -509,6 +525,7 @@
             pltpu.VMEM((SIDE, 384), BF),
             pltpu.VMEM((8, SIDE, 2 * SIDE), F),
             pltpu.VMEM((SIDE, SIDE), F),
+            pltpu.VMEM((SIDE, SIDE), BF),
             pltpu.VMEM((4, SIDE, SIDE), F),
             pltpu.VMEM((4, SIDE, SIDE), F),
             pltpu.SMEM(taps.shape, F),
@@ -529,65 +546,35 @@
     )(*[pltpu.with_memory_space_constraint(a, pltpu.HBM) for a in (taps, ranks)], probes)
 
 
-CHUNKS = 8
-
-
-def basis_kernel(sketch, weights_ref, moved, out, moved_out, result, store_sem, pass_sem):
-    rows = SIDE // CHUNKS
-
-    def store(index):
+def store_kernel(basis, moved, basis_out, moved_out, sems):
+    rows = SIDE // 8
+    copies = [pltpu.make_async_copy(moved, moved_out, sems.at[8])]
+    for index in range(8):
         here = pl.ds(rows * index, rows)
-        return pltpu.make_async_copy(result.at[here], out.at[here], store_sem.at[index])
-
-    forward = pltpu.make_async_copy(moved, moved_out, pass_sem)
-    forward.start()
-    weights = weights_ref[...]
-    zero = jnp.zeros_like(weights)
-    twice = jnp.concatenate(
-        [jnp.concatenate([weights, zero], axis=1), jnp.concatenate([zero, weights], axis=1)], axis=0
-    )
-
-    @pl.loop(0, CHUNKS)
-    def _(index):
-        half = rows // 2
-        base = rows * index
-        pair = [
-            sketch[pl.ds(base + half * k, half)].reshape(half * SIDE, SIDE) for k in range(2)
-        ]
-        both = jnp.dot(jnp.concatenate(pair, axis=1), twice, preferred_element_type=F).astype(BF)
-        for k in range(2):
-            result[pl.ds(base + half * k, half)] = both[:, SIDE * k : SIDE * (k + 1)].reshape(
-                half, SIDE, SIDE
-            )
-        store(index).start()
-
-    for index in range(CHUNKS):
-        store(index).wait()
-    forward.wait()
-
-
-def basis(sketch, weights, moved):
+        copies.append(pltpu.make_async_copy(basis.at[here], basis_out.at[here], sems.at[index]))
+    for copy in copies:
+        copy.start()
+    for copy in copies:
+        copy.wait()
+
+
+def store(basis, moved):
     return pl.pallas_call(
-        basis_kernel,
+        store_kernel,
         out_shape=(
-            jax.ShapeDtypeStruct(sketch.shape, BF),
+            jax.ShapeDtypeStruct(basis.shape, BF),
             jax.ShapeDtypeStruct(moved.shape, F),
         ),
-        in_specs=[pl.BlockSpec(memory_space=pltpu.VMEM)] * 3,
+        in_specs=[pl.BlockSpec(memory_space=pltpu.VMEM)] * 2,
         out_specs=(pl.BlockSpec(memory_space=pltpu.HBM),) * 2,
-        scratch_shapes=[
-            pltpu.VMEM(sketch.shape, BF),
-            pltpu.SemaphoreType.DMA((CHUNKS,)),
-            pltpu.SemaphoreType.DMA,
-        ],
+        scratch_shapes=[pltpu.SemaphoreType.DMA((9,))],
         compiler_params=pltpu.CompilerParams(vmem_limit_bytes=16 * 2**20),
-        name="basis",
-    )(sketch, weights, moved)
+        name="store",
+    )(basis, moved)
 
 
 def local(probes, filter_taps, cluster_ranks):
-    sketch, weights, moved = compress(filter_taps, jnp.swapaxes(cluster_ranks, 1, 2), probes)
-    return basis(sketch, weights, moved)
+    return store(*compress(filter_taps, jnp.swapaxes(cluster_ranks, 1, 2), probes))
 
 
 def solution(mesh):

time: 103 us -> 102 us (level)
    pallas_call x1, Pallas kernels: 3.29 us -> 2.17 us  [store(): pl.pallas_call(store_kernel, out_shape=(jax.ShapeDtypeStruct(basis.shape,...]
where the time goes in v7:
time: 102 us
  Pallas kernels  101 us (99%)
    pallas_call x1, Pallas kernels, compress(): pl.pallas_call(body, out_shape=(jax.ShapeDtypeStruct((SIDE, SIDE, SIDE),...  99.1 us
    pallas_call x1, Pallas kernels, store(): pl.pallas_call(store_kernel, out_shape=(jax.ShapeDtypeStruct(basis.shape,...  2.17 us

profile of v7, /device:TPU:96, one launch (start us, length us, event | category | flops | bytes accessed | tf_op | source)
XLA Modules:
  0.0 101.9 jit_solution(13204083910157609868)
XLA Ops:
  0.6 99.1 %compress.1 = (bf16[128,128,128]{2,1,0:T(8,128)(2,1)S(1)}, f32[1,1,4,128,128]{4,3,2,1,0:T(8,128)S(1)}) custom-call(f32[2,2,33]{2,1,0:T(2,128)} %taps_far.1, s32[5,8,32]{2,1,0:T(8,128)} %bitcast.1, bf16[128,128,128]{2,1,0:T(8,128)(2,1)} %probes.1), custom_call_target="tpu_custom_call" | custom-call | tf_op jit(solution)/shard_map/compress/pallas_call | solution.py:509
  99.7 2.2 %store.1 = (bf16[128,128,128]{2,1,0:T(8,128)(2,1)}, f32[1,1,4,128,128]{4,3,2,1,0:T(8,128)}) custom-call(bf16[128,128,128]{2,1,0:T(8,128)(2,1)S(1)} %get-tuple-element.4.basis, f32[1,1,4,128,128]{4,3,2,1,0:T(8,128)S(1)} %get-tuple-element.5.moved), custom_call_target="tpu_custom_call" | custom-call | tf_op jit(solution)/shard_map/store/pallas_call | solution.py:562

commit v8 on v7

--- a/solution.py
+++ b/solution.py
@@ -425,8 +425,10 @@
         filter_cols(step)
         each(sent, step)
 
+    pieces = ((0, 48), (48, 48), (96, 16), (112, 16))
+
     def swap(level, b):
-        here = pl.ds(16 * b, 16)
+        here = pl.ds(*pieces[b])
         return pltpu.make_async_remote_copy(
             src_ref=own.at[level, here],
             dst_ref=other.at[level, here],
@@ -448,7 +450,9 @@
 
         def emit(b, solved):
             own[level, 16 * b : 16 * b + 16] = solved
-            swap(level, b).start()
+            for index, (first, count) in enumerate(pieces):
+                if 16 * b + 16 == first + count:
+                    swap(level, index).start()
 
         linv = factor(gram_ref[...], rank_at(level, span_x, span_y), emit)
 
@@ -476,17 +480,20 @@
                 sketch[pl.ds(rows + 4 * k, 4)] = (
                     both[:, SIDE * k : SIDE * (k + 1)].astype(BF).reshape(4, SIDE, SIDE)
                 )
-        for b in range(8):
+        for b in range(3):
             swap(level, b).wait_recv()
-        both = jnp.concatenate([own[level], other[level]], axis=0)
-        gram_ref[...] = dot_tn(both, both) * 0.5
+        most = jnp.concatenate([own[level], other[level, 0:112]], axis=0)
+        gram_ref[...] = dot_tn(most, most)
+        swap(level, 3).wait_recv()
+        rest = other[level, 112:128]
+        gram_ref[...] = (gram_ref[...] + dot_tn(rest, rest)) * 0.5
 
     linv = factor(gram_ref[...], rank_at(4, 4, 4))
     moved_ref[0, 0, 3] = dot_nt(own[3], linv)
 
     @pl.loop(0, 4)
     def _(level):
-        for b in range(8):
+        for b in range(4):
             swap(level, b).wait_send()
 
     def sent_cols(step):
@@ -536,8 +543,8 @@
             pltpu.SemaphoreType.DMA((2, STEPS + 1)),
             pltpu.SemaphoreType.DMA((2, 2, STEPS + 1)),
             pltpu.SemaphoreType.DMA((2, 2, STEPS + 1)),
-            pltpu.SemaphoreType.DMA((4, 8)),
-            pltpu.SemaphoreType.DMA((4, 8)),
+            pltpu.SemaphoreType.DMA((4, 4)),
+            pltpu.SemaphoreType.DMA((4, 4)),
         ],
         compiler_params=pltpu.CompilerParams(
             collective_id=0, has_side_effects=True, vmem_limit_bytes=48 * 2**20

time: 102 us -> 103 us (level)
  no operation moved by 1% of the time
where the time goes in v8:
time: 103 us
  Pallas kernels  102 us (99%)
    pallas_call x1, Pallas kernels, compress(): pl.pallas_call(body, out_shape=(jax.ShapeDtypeStruct((SIDE, SIDE, SIDE),...  99.9 us
    pallas_call x1, Pallas kernels, store(): pl.pallas_call(store_kernel, out_shape=(jax.ShapeDtypeStruct(basis.shape,...  2.17 us

profile of v8, /device:TPU:96, one launch (start us, length us, event | category | flops | bytes accessed | tf_op | source)
XLA Modules:
  0.0 102.8 jit_solution(17070166351628763450)
XLA Ops:
  0.6 99.9 %compress.1 = (bf16[128,128,128]{2,1,0:T(8,128)(2,1)S(1)}, f32[1,1,4,128,128]{4,3,2,1,0:T(8,128)S(1)}) custom-call(f32[2,2,33]{2,1,0:T(2,128)} %taps_far.1, s32[5,8,32]{2,1,0:T(8,128)} %bitcast.1, bf16[128,128,128]{2,1,0:T(8,128)(2,1)} %probes.1), custom_call_target="tpu_custom_call" | custom-call | tf_op jit(solution)/shard_map/compress/pallas_call | solution.py:516
  100.6 2.2 %store.1 = (bf16[128,128,128]{2,1,0:T(8,128)(2,1)}, f32[1,1,4,128,128]{4,3,2,1,0:T(8,128)}) custom-call(bf16[128,128,128]{2,1,0:T(8,128)(2,1)S(1)} %get-tuple-element.4.basis, f32[1,1,4,128,128]{4,3,2,1,0:T(8,128)S(1)} %get-tuple-element.5.moved), custom_call_target="tpu_custom_call" | custom-call | tf_op jit(solution)/shard_map/store/pallas_call | solution.py:569
